TPU v7x, 512 devices: a whole 4x8x8 slice. The times are simulated.
512 devices in a mesh: src: 16 (over z, core), row: 32 (over x, y).
Axes of the slice: x: 4, y: 8, z: 8, core: 2. Of those that a mesh axis runs over, the one named last changes fastest.
Arguments:
- spec_re: bfloat16 [1024, 1024], P('row'), may hold values from -18 to 18
- spec_im: bfloat16 [1024, 1024], P('row'), may hold values from -18 to 18
- target: float32 [1024, 1024], P('row'), may hold values from 0.3 to 1.5
- weights: float32 [128], P('src'), may hold values from 0.25 to 2.5
- cent_row: int32 [128], P('src'), may hold values from 128 to 895
- cent_col: int32 [128], P('src'), may hold values from 128 to 895
Outputs:
- grad_re: float32 [1024, 1024], P('row')
- grad_im: float32 [1024, 1024], P('row')
Inputs may be any that keep to these rules, and one draw needn't show every extreme that they name: Every pupil disk of radius 128 about (cent_row, cent_col) lies inside the band.
All inputs are finite; a program needn't handle non-finite values.
Results may differ from a plain program's by a relative error of at most 0.0072.
Values may be sent and summed in bfloat16 or wider, within the bound.
No kernel may reach another device: no remote copies, remote signals or barrier semaphores. Data moves between devices by JAX's collectives and lax.ppermute only.
A program may use at most 128 MiB of HBM per device.

v0:
```python
import math

import jax
import jax.numpy as jnp
from jax import lax
from jax.sharding import PartitionSpec as P

RAD = 128
WIN = 384


def make_tables(band):
    position = jnp.arange(band, dtype=jnp.int32)
    phase = position[:, None] * position[None, :] % band
    angle = phase.astype(jnp.float32) * (2.0 * math.pi / band)
    factor = 1.0 / math.sqrt(band)
    return (
        (jnp.cos(angle) * factor).astype(jnp.bfloat16),
        (jnp.sin(angle) * factor).astype(jnp.bfloat16),
    )


def local(spec_re, spec_im, target, weights, cent_row, cent_col):
    rows_dev, band = spec_re.shape
    cols_dev = target.shape[0]
    points_dev = weights.shape[0]
    total_points = points_dev * lax.axis_size("src")
    cosine, sine = make_tables(band)
    tables_joined = jnp.concatenate([cosine, sine], axis=1)
    row_first = lax.axis_index("row") * rows_dev
    window_index = jnp.arange(WIN, dtype=jnp.int32)
    zero_value = jnp.zeros((), jnp.bfloat16)
    stacked = jnp.stack([spec_re, spec_im], axis=0)

    def window_starts(centre_cols):
        return jnp.clip(centre_cols - RAD, 0, band - WIN)

    def disk_window(first_row, row_count, centre_rows, centre_cols, starts):
        rows_here = first_row + jnp.arange(row_count, dtype=jnp.int32)
        row_gap = rows_here[None, :] - centre_rows[:, None]
        col_gap = starts[:, None] + window_index[None, :] - centre_cols[:, None]
        return row_gap[:, :, None] ** 2 + col_gap[:, None, :] ** 2 <= RAD * RAD

    col_first = lax.axis_index("row") * cols_dev
    narrow = jnp.concatenate(
        [
            lax.dynamic_slice_in_dim(cosine, col_first, cols_dev, 1),
            lax.dynamic_slice_in_dim(sine, col_first, cols_dev, 1),
        ],
        axis=1,
    )
    starts_all = window_starts(cent_col)
    narrow_windows = jax.vmap(lambda start: lax.dynamic_slice_in_dim(narrow, start, WIN, 0))(
        starts_all
    )
    spectrum_piece = lax.all_gather(stacked, "row", axis=1, tiled=True)
    inside_disk = disk_window(jnp.int32(0), spectrum_piece.shape[1], cent_row, cent_col, starts_all)
    pieces = jax.vmap(lambda start: lax.dynamic_slice_in_dim(spectrum_piece, start, WIN, 2))(
        starts_all
    )
    masked = jnp.where(inside_disk[:, None], pieces, zero_value)
    product = jnp.einsum(
        "pckl,plz->pckz", masked, narrow_windows, preferred_element_type=jnp.float32
    )
    real_part = product[:, 0, :, :cols_dev] - product[:, 1, :, cols_dev:]
    imag_part = product[:, 0, :, cols_dev:] + product[:, 1, :, :cols_dev]
    received = jnp.stack([real_part, imag_part], axis=1).astype(jnp.bfloat16)
    product = jnp.einsum(
        "pcky,kz->pcyz", received, tables_joined, preferred_element_type=jnp.float32
    )
    field_re = product[:, 0, :, :band] - product[:, 1, :, band:]
    field_im = product[:, 0, :, band:] + product[:, 1, :, :band]
    field = jnp.stack([field_re, field_im], axis=1)
    power = field[:, 0] * field[:, 0] + field[:, 1] * field[:, 1]
    local_power = jnp.sum(weights[:, None, None] * power, axis=0) / total_points
    intensity = lax.psum(local_power, "src")
    mismatch = intensity - target
    grad_field = (2.0 * weights[:, None, None, None] * mismatch[None, None] * field).astype(
        jnp.bfloat16
    )
    product = jnp.einsum(
        "pcyx,xz->pcyz", grad_field, tables_joined, preferred_element_type=jnp.float32
    )
    adj_re = product[:, 0, :, :band] + product[:, 1, :, band:]
    adj_im = product[:, 1, :, :band] - product[:, 0, :, band:]
    adjoint = jnp.stack([adj_re, adj_im], axis=1).astype(jnp.bfloat16)
    returned = lax.all_to_all(adjoint, "row", split_axis=3, concat_axis=2, tiled=True)
    starts = window_starts(cent_col)
    inside_disk = disk_window(row_first, rows_dev, cent_row, cent_col, starts)
    col_tables = jax.vmap(
        lambda start: jnp.concatenate(
            [
                lax.dynamic_slice_in_dim(cosine, start, WIN, 1),
                lax.dynamic_slice_in_dim(sine, start, WIN, 1),
            ],
            axis=1,
        )
    )(starts)
    result = jnp.einsum("pcyk,pyz->pckz", returned, col_tables, preferred_element_type=jnp.float32)
    term_re = result[:, 0, :, :WIN] + result[:, 1, :, WIN:]
    term_im = result[:, 1, :, :WIN] - result[:, 0, :, WIN:]
    zero_float = jnp.zeros((), jnp.float32)
    terms_re = jnp.where(inside_disk, term_re, zero_float)
    terms_im = jnp.where(inside_disk, term_im, zero_float)
    starts_local = window_starts(cent_col)
    local_re = jnp.zeros((rows_dev, band), jnp.float32)
    local_im = jnp.zeros((rows_dev, band), jnp.float32)
    for point in range(points_dev):
        start = starts_local[point]
        old_re = lax.dynamic_slice_in_dim(local_re, start, WIN, 1)
        old_im = lax.dynamic_slice_in_dim(local_im, start, WIN, 1)
        local_re = lax.dynamic_update_slice_in_dim(local_re, old_re + terms_re[point], start, 1)
        local_im = lax.dynamic_update_slice_in_dim(local_im, old_im + terms_im[point], start, 1)
    grad_re, grad_im = lax.psum((local_re, local_im), "src")
    return (grad_re, grad_im)


def solution(mesh):
    return jax.shard_map(
        local,
        mesh=mesh,
        in_specs=(P("row", None), P("row", None), P("row", None), P("src"), P("src"), P("src")),
        out_specs=(P("row", None), P("row", None)),
        check_vma=False,
    )
```

profile of v0, /device:TPU:1, one launch (start us, length us, event | category | flops | bytes accessed | tf_op | source)
XLA Modules:
  0.0 503.4 jit_solution(15990547782452756728)
XLA Ops:
  9.6 15.8 %multiply_convert_fusion = bf16[1024,1024]{1,0:T(8,128)(2,1)S(1)} fusion(), kind=kLoop, calls=%fused_computation.23 | loop fusion | flops 16777216 | bytes 2097152 | tf_op jit(solution)/shard_map/convert_element_type | solution.py:19
  25.4 15.7 %multiply_convert_fusion.1 = bf16[1024,1024]{1,0:T(8,128)(2,1)S(1)} fusion(), kind=kLoop, calls=%fused_computation.24 | loop fusion | flops 16777216 | bytes 2097152 | tf_op jit(solution)/shard_map/convert_element_type | solution.py:18
  41.8 3.6 add_compare_fusion
  45.4 9.6 %while.9 = (s32[]{:T(128)}, bf16[1024,64]{1,0:T(8,128)(2,1)S(1)}, s32[8,2]{0,1:T(2,128)S(1)}, bf16[8,384,64]{2,1,0:T(8,128)(2,1)S(1)}) while((s32[]{:T(128)}, bf16[1024,64]{1,0:T(8,128)(2,1)S(1)}, s32[8,2]{0,1:T(2,128)S(1)}, bf16[8,384,64]{2,1,0:T(8,128)(2,1)S(1)}) %tuple.83), condition=%wide.while_cond.1.clone, body=%wide.while_body.1.sunk.clone | while | flops 2 | bytes 196705 | solution.py:53
  58.2 30.4 %while.11 = (s32[]{:T(128)}, bf16[1024,1024]{1,0:T(8,128)(2,1)}, s32[8,2]{0,1:T(2,128)S(1)}, bf16[8,1024,384]{2,1,0:T(8,128)(2,1)}) while((s32[]{:T(128)}, bf16[1024,1024]{1,0:T(8,128)(2,1)}, s32[8,2]{0,1:T(2,128)S(1)}, bf16[8,1024,384]{2,1,0:T(8,128)(2,1)}) %tuple.100), condition=%wide.while_cond.3.clone, body=%wide.while_body.3.sunk.clone | while | flops 2 | bytes 1573469 | solution.py:94
  58.8 3.2 bitcast_dynamic-update-slice_fusion.15
  66.4 3.1 bitcast_dynamic-update-slice_fusion.15
  70.2 3.2 bitcast_dynamic-update-slice_fusion.15
  85.4 3.2 bitcast_dynamic-update-slice_fusion.15
  88.5 12.3 %all-gather.2.cloned.1.call-done = bf16[2,1024,1024]{2,1,0:T(8,128)(2,1)} async-done(((bf16[2,32,1024]{2,1,0:T(8,128)(2,1)}), bf16[2,1024,1024]{2,1,0:T(8,128)(2,1)}) %all-gather.2.cloned.1.call-update) | async-done | bytes 4194320 | tf_op jit(solution)/shard_map/all_gather | solution.py:56
  100.8 37.9 %while.8 = (s32[]{:T(128)}, bf16[2,1024,1024]{2,1,0:T(8,128)(2,1)}, s32[8,3]{0,1:T(4,128)S(1)}, bf16[8,2,1024,384]{3,2,1,0:T(8,128)(2,1)}) while((s32[]{:T(128)}, bf16[2,1024,1024]{2,1,0:T(8,128)(2,1)}, s32[8,3]{0,1:T(4,128)S(1)}, bf16[8,2,1024,384]{3,2,1,0:T(8,128)(2,1)}) %tuple.80), condition=%wide.while_cond.clone, body=%wide.while_body.sunk.clone | while | flops 2 | bytes 3146341 | solution.py:58
  101.4 4.2 bitcast_dynamic-update-slice_fusion.12
  106.1 4.2 bitcast_dynamic-update-slice_fusion.12
  110.9 4.2 bitcast_dynamic-update-slice_fusion.12
  115.6 4.2 bitcast_dynamic-update-slice_fusion.12
  120.4 4.1 bitcast_dynamic-update-slice_fusion.12
  125.1 4.1 bitcast_dynamic-update-slice_fusion.12
  129.8 4.2 bitcast_dynamic-update-slice_fusion.12
  134.5 4.2 bitcast_dynamic-update-slice_fusion.12
  138.7 7.7 %fusion = f32[8,2,1024,64]{2,3,1,0:T(8,128)S(1)} fusion(bf16[8,2,1024,384]{3,2,1,0:T(8,128)(2,1)} %get-tuple-element.9, pred[8,1024,384]{2,1,0:T(8,128)(4,1)} %add_compare_fusion, bf16[8,384,64]{2,1,0:T(8,128)(2,1)S(1)} %get-tuple-element.17), kind=kOutput, calls=%fused_computation.9 | convolution fusion | flops 811597824 | bytes 20316160 | tf_op jit(solution)/shard_map/pckl,plz->pckz/dot_general | solution.py:62
  152.7 117.0 %all-reduce.7.cloned.1.call-done = f32[32,1024]{1,0:T(8,128)} async-done(((f32[32,1024]{1,0:T(8,128)}), f32[32,1024]{1,0:T(8,128)}) %all-reduce.7.cloned.1.call-update) | async-done | bytes 131088 | tf_op jit(solution)/shard_map/psum | solution.py:76
  270.8 4.3 fusion.11
  275.5 7.5 %copy.13 = bf16[8,2,32,1024]{2,1,0,3:T(2,128)(2,1)} copy(bf16[8,2,32,1024]{3,2,1,0:T(8,128)(2,1)S(1)} %pad_maximum_fusion) | data formatting | bytes 2097152 | tf_op jit(solution)/shard_map/stack | solution.py:86
  283.1 9.9 %reshape.192 = bf16[32,2,8192]{2,1,0:T(2,128)(2,1)} reshape(bf16[1024,8,2,32]{3,2,1,0:T(2,128)(2,1)} %bitcast.159) | data formatting | bytes 2097152
  293.0 9.3 %all-to-all-start = ((bf16[32,2,8192]{2,1,0:T(2,128)(2,1)}), bf16[32,2,8192]{2,1,0:T(2,128)(2,1)S(1)}, u32[]{:S(2)}, u32[]{:S(2)}) async-start(bf16[32,2,8192]{2,1,0:T(2,128)(2,1)} %reshape.192), calls=%async_computation | async-start | bytes 2097152 | tf_op jit(solution)/shard_map/all_to_all | solution.py:87
  318.0 3.2 broadcast.133.clone.1
  321.2 20.0 %while.10 = (s32[]{:T(128)}, bf16[1024,1024]{1,0:T(8,128)(2,1)S(1)}, s32[8,2]{0,1:T(2,128)S(1)}, bf16[8,1024,384]{2,1,0:T(8,128)(2,1)}) while((s32[]{:T(128)}, bf16[1024,1024]{1,0:T(8,128)(2,1)S(1)}, s32[8,2]{0,1:T(2,128)S(1)}, bf16[8,1024,384]{2,1,0:T(8,128)(2,1)}) %tuple.101), condition=%wide.while_cond.2.clone, body=%wide.while_body.2.sunk.clone | while | flops 2 | bytes 1573469 | solution.py:93
  341.2 3.6 reshape.193
  344.8 6.9 %copy.25 = bf16[8,2,32,32,32]{2,3,4,1,0:T(8,128)(2,1)} copy(bf16[8,2,32,32,32]{2,1,0,4,3:T(2,128)(2,1)} %bitcast.160) | data formatting | bytes 2097152 | tf_op jit(solution)/shard_map/all_to_all | solution.py:87
  351.7 6.2 %all_to_all.16 = bf16[8,2,1024,32]{2,3,1,0:T(8,128)(2,1)S(1)} reshape(bf16[8,2,32,32,32]{3,2,4,1,0:T(8,128)(2,1)} %bitcast.161) | data formatting | bytes 2097152 | tf_op jit(solution)/shard_map/all_to_all | solution.py:87
  357.9 5.8 %fusion.2 = f32[8,2,32,768]{3,2,1,0:T(8,128)S(1)} fusion(bf16[8,2,1024,32]{2,3,1,0:T(8,128)(2,1)S(1)} %all_to_all.16, bf16[8,1024,384]{2,1,0:T(8,128)(2,1)} %get-tuple-element.33, bf16[8,1024,384]{2,1,0:T(8,128)(2,1)} %get-tuple-element.25), kind=kOutput, calls=%fused_computation.12 | convolution fusion | flops 830472192 | bytes 15204352 | tf_op jit(solution)/shard_map/pcyk,pyz->pckz/dot_general | solution.py:99
  376.4 117.4 %all-reduce.9.cloned.1.call-done = (f32[32,1024]{1,0:T(8,128)}, f32[32,1024]{1,0:T(8,128)}) async-done(((f32[32,1024]{1,0:T(8,128)}, f32[32,1024]{1,0:T(8,128)}), (f32[32,1024]{1,0:T(8,128)}, f32[32,1024]{1,0:T(8,128)})) %all-reduce.9.cloned.1.call-update) | async-done | bytes 262160 | tf_op jit(solution)/shard_map/psum | solution.py:114
  (167 shorter events, 81.9 us)
Async XLA Ops:
  7.2 34.5 %copy-start.7 = (s32[8]{0:T(128)S(1)}, s32[8]{0:T(128)}, u32[]{:S(2)}) copy-start(s32[8]{0:T(128)} %param.11) | copy-start | bytes 100
  7.2 34.4 %copy-start.5 = (s32[8]{0:T(128)S(1)}, s32[8]{0:T(128)}, u32[]{:S(2)}) copy-start(s32[8]{0:T(128)} %param.10) | copy-start | bytes 100
  7.2 93.6 %all-gather.2.cloned.1.call-start = ((), (), s32[]{:S(2)}) async-start(), calls=%async_computation.1 | async-start | bytes 4325376 | tf_op jit(solution)/shard_map/all_gather | solution.py:56
  8.8 260.9 %all-reduce.7.cloned.1.call-start = ((), (), s32[]{:S(2)}) async-start(), calls=%async_computation.2 | async-start | bytes 262144 | tf_op jit(solution)/shard_map/psum | solution.py:76
  25.4 15.7 %copy-start = (bf16[1024,1024]{1,0:T(8,128)(2,1)}, bf16[1024,1024]{1,0:T(8,128)(2,1)S(1)}, u32[]{:S(2)}) copy-start(bf16[1024,1024]{1,0:T(8,128)(2,1)S(1)} %multiply_convert_fusion) | copy-start | bytes 6291460
  146.4 1.6 copy-start.1
  148.0 2.4 copy-start.6
  150.4 119.3 %copy-start.4 = (f32[32,1024]{1,0:T(8,128)S(1)}, f32[32,1024]{1,0:T(8,128)}, u32[]{:S(2)}) copy-start(f32[32,1024]{1,0:T(8,128)} %param.8) | copy-start | bytes 393220
  293.0 48.2 %all-to-all-start = ((bf16[32,2,8192]{2,1,0:T(2,128)(2,1)}), bf16[32,2,8192]{2,1,0:T(2,128)(2,1)S(1)}, u32[]{:S(2)}, u32[]{:S(2)}) async-start(bf16[32,2,8192]{2,1,0:T(2,128)(2,1)} %reshape.192), calls=%async_computation | async-start | bytes 2097152 | tf_op jit(solution)/shard_map/all_to_all | solution.py:87
  302.3 191.5 %all-reduce.9.cloned.1.call-start = ((), (), s32[]{:S(2)}) async-start(), calls=%async_computation.3 | async-start | bytes 524288 | tf_op jit(solution)/shard_map/psum | solution.py:114
  369.8 5.9 %copy-start.3 = (f32[32,1024]{1,0:T(8,128)}, f32[32,1024]{1,0:T(8,128)S(1)}, u32[]{:S(2)}) copy-start(f32[32,1024]{1,0:T(8,128)S(1)} %dynamic_update_slice.55) | copy-start | bytes 393220
  375.7 0.7 copy-start.2
Sparse Core Ops, SparseCore 0:
  11.7 88.9 all-gather.1
  152.8 116.8 all-reduce.6
  376.5 117.2 all-reduce.8
where the time goes:
time: 505 us; the launch traced here: 503 us
  waiting for transfers between devices  247 us (49%)
  local copies, waits for them, and re-layouts  154 us (30%)
  other arithmetic  43.3 us (9%)
  between operations  29.3 us (6%)
  matrix products  20.2 us (4%)
  starting transfers between devices  9.38 us (2%)
    psum x1, waiting for transfers between devices, local(): grad_re, grad_im = lax.psum((local_re, local_im), 'src')  117 us
    psum x1, waiting for transfers between devices, local(): intensity = lax.psum(local_power, 'src')  117 us
    gather x96, local copies, waits for them, and re-layouts  97.7 us
    unnamed x22, local copies, waits for them, and re-layouts  24.9 us
    convert_element_type x1, other arithmetic, make_tables(): (jnp.sin(angle) * factor).astype(jnp.bfloat16)  15.8 us
    convert_element_type x1, other arithmetic, make_tables(): (jnp.cos(angle) * factor).astype(jnp.bfloat16)  15.7 us
    all_to_all x2, local copies, waits for them, and re-layouts, local(): lax.all_to_all(adjoint, 'row', split_axis=3, concat_axis=2, tiled=True)  13.1 us
    all_gather x1, waiting for transfers between devices, local(): spectrum_piece = lax.all_gather(stacked, 'row', axis=1, tiled=True)  12.3 us
  transfers between devices with their start and end apart: 4, of which 3 were waited for; matrix products, arithmetic and copies ran while one was open for 21% of the time, Pallas kernels for 0%

commit v1 on v0

v1 whole, which is shorter than its diff:
```python
import functools
import math

import jax
import jax.numpy as jnp
from jax import lax
from jax.experimental import pallas as pl
from jax.experimental.pallas import tpu as pltpu
from jax.sharding import PartitionSpec as P

RAD = 128
F32 = jnp.float32
BF16 = jnp.bfloat16
CHUNK = 256
LANES = 128

WHOLE = pl.BlockSpec(memory_space=pltpu.VMEM)
SCALARS = pl.BlockSpec(memory_space=pltpu.SMEM)


def trig_rows(band):
    index = jnp.arange(32, dtype=jnp.int32)
    rows = jnp.where(index < 16, 64 * index, jnp.where(index < 24, 8 * (index - 16), index - 24))
    phase = rows[:, None] * jnp.arange(band, dtype=jnp.int32)[None, :]
    both = jnp.concatenate([phase, phase + (band - band // 4)], axis=0) % band
    return jnp.cos(both.astype(F32) * (2.0 * math.pi / band))


def inside(first_row, first_col, shape, centre_row, centre_col):
    row_gap = lax.broadcasted_iota(jnp.int32, shape, 0) + (first_row - centre_row)
    col_gap = lax.broadcasted_iota(jnp.int32, shape, 1) + (first_col - centre_col)
    return row_gap * row_gap + col_gap * col_gap <= RAD * RAD


def scatter_blocks(product, out_ref):
    group = lax.broadcasted_iota(jnp.int32, (32, LANES), 1) // 32
    for tile in range(CHUNK // LANES):
        for quad in range(4):
            rows = [
                product[32 * (4 * quad + j) : 32 * (4 * quad + j) + 32, tile * LANES : (tile + 1) * LANES]
                for j in range(4)
            ]
            for dest in range(4):
                joined = None
                for j in range(4):
                    shift = (32 * (j - dest)) % LANES
                    moved = pltpu.roll(rows[j], shift, 1) if shift else rows[j]
                    joined = moved if joined is None else jnp.where(group == j, moved, joined)
                out_ref[4 * tile + dest, :, quad * LANES : (quad + 1) * LANES] = joined.astype(BF16)


def spectrum_kernel(row_ref, cr_ref, cc_ref, trig_ref, re_ref, im_ref, cos_ref, sin_ref, out_ref, lhs_ref):
    step = pl.program_id(0)
    rows, band = re_ref.shape
    points = cr_ref.shape[0]
    half = rows * points

    @pl.when(step == 0)
    def _():
        spec_re = re_ref[...].astype(F32)
        spec_im = im_ref[...].astype(F32)
        for p in range(points):
            keep = inside(row_ref[0] * rows, 0, (rows, band), cr_ref[p], cc_ref[p])
            part_re = jnp.where(keep, spec_re, 0.0)
            part_im = jnp.where(keep, spec_im, 0.0)
            top = slice(p * rows, (p + 1) * rows)
            low = slice(half + p * rows, half + (p + 1) * rows)
            lhs_ref[top, :band] = part_re.astype(BF16)
            lhs_ref[low, band:] = part_re.astype(BF16)
            lhs_ref[low, :band] = part_im.astype(BF16)
            lhs_ref[top, band:] = (-part_im).astype(BF16)

    scale = 1.0 / math.sqrt(band)
    fine_c, fine_s = trig_ref[24:32, :], trig_ref[56:64, :]
    base_c, base_s = [], []
    for b in range(8):
        c, s = trig_ref[16 + b : 17 + b, :], trig_ref[48 + b : 49 + b, :]
        base_c.append((c * fine_c - s * fine_s) * scale)
        base_s.append((s * fine_c + c * fine_s) * scale)
    base_c = jnp.concatenate(base_c, axis=0)
    base_s = jnp.concatenate(base_s, axis=0)
    for a in range(16):
        c, s = trig_ref[a : a + 1, :], trig_ref[32 + a : 33 + a, :]
        cos_ref[64 * a : 64 * a + 64, :] = (c * base_c - s * base_s).astype(BF16)
        sin_ref[64 * a : 64 * a + 64, :] = (s * base_c + c * base_s).astype(BF16)
    product = jnp.dot(lhs_ref[:, :band], cos_ref[...], preferred_element_type=F32)
    product += jnp.dot(lhs_ref[:, band:], sin_ref[...], preferred_element_type=F32)
    scatter_blocks(product, out_ref)


def field_kernel(w_ref, in_ref, cos_ref, sin_ref, field_ref, power_ref, lhs_ref):
    band = in_ref.shape[0]
    half = in_ref.shape[1] // 2
    points = w_ref.shape[0]
    rows = half // points

    @pl.when(pl.program_id(0) == 0)
    def _():
        for k in range(0, band, CHUNK):
            turned = in_ref[k : k + CHUNK, :].T
            lhs_ref[:, k : k + CHUNK] = turned
            lhs_ref[:half, band + k : band + k + CHUNK] = -turned[half:]
            lhs_ref[half:, band + k : band + k + CHUNK] = turned[:half]

    product = jnp.dot(lhs_ref[:, :band], cos_ref[...], preferred_element_type=F32)
    product += jnp.dot(lhs_ref[:, band:], sin_ref[...], preferred_element_type=F32)
    field_ref[...] = product
    total = jnp.zeros((rows, CHUNK), F32)
    for p in range(points):
        re = product[p * rows : (p + 1) * rows]
        im = product[half + p * rows : half + (p + 1) * rows]
        total += w_ref[p] * (re * re + im * im)
    for block in range(4):
        for side in range(2):
            power_ref[block, 0, 8 * side : 8 * side + 8, :] = total[
                8 * block : 8 * block + 8, side * LANES : (side + 1) * LANES
            ]


def adjoint_kernel(total_points, w_ref, power_ref, target_ref, field_ref, cos_ref, sin_ref, out_ref, lhs_ref):
    rows, band = target_ref.shape
    points = w_ref.shape[0]
    half = rows * points

    @pl.when(pl.program_id(0) == 0)
    def _():
        for n in range(4):
            cols = slice(n * CHUNK, (n + 1) * CHUNK)
            power = jnp.concatenate(
                [
                    jnp.concatenate([power_ref[block, n, :8, :], power_ref[block, n, 8:, :]], axis=1)
                    for block in range(4)
                ],
                axis=0,
            )
            mismatch = power * (1.0 / total_points) - target_ref[:, cols]
            shifted = slice(band + n * CHUNK, band + (n + 1) * CHUNK)
            for p in range(points):
                top = slice(p * rows, (p + 1) * rows)
                low = slice(half + p * rows, half + (p + 1) * rows)
                factor = (2.0 * w_ref[p]) * mismatch
                grad_re = factor * field_ref[top, cols]
                grad_im = factor * field_ref[low, cols]
                lhs_ref[top, cols] = grad_re.astype(BF16)
                lhs_ref[top, shifted] = grad_im.astype(BF16)
                lhs_ref[low, cols] = grad_im.astype(BF16)
                lhs_ref[low, shifted] = (-grad_re).astype(BF16)

    product = jnp.dot(lhs_ref[:, :band], cos_ref[...], preferred_element_type=F32)
    product += jnp.dot(lhs_ref[:, band:], sin_ref[...], preferred_element_type=F32)
    scatter_blocks(product, out_ref)


def gradient_kernel(row_ref, cr_ref, cc_ref, in_ref, cos_ref, sin_ref, out_ref, lhs_ref):
    step = pl.program_id(0)
    band = in_ref.shape[0]
    half = in_ref.shape[1] // 2
    points = cr_ref.shape[0]
    rows = half // points

    @pl.when(step == 0)
    def _():
        for k in range(0, band, CHUNK):
            turned = in_ref[k : k + CHUNK, :].T
            lhs_ref[:, k : k + CHUNK] = turned
            lhs_ref[:half, band + k : band + k + CHUNK] = turned[half:]
            lhs_ref[half:, band + k : band + k + CHUNK] = -turned[:half]

    product = jnp.dot(lhs_ref[:, :band], cos_ref[...], preferred_element_type=F32)
    product += jnp.dot(lhs_ref[:, band:], sin_ref[...], preferred_element_type=F32)
    total_re = jnp.zeros((rows, CHUNK), F32)
    total_im = jnp.zeros((rows, CHUNK), F32)
    for p in range(points):
        keep = inside(row_ref[0] * rows, step * CHUNK, (rows, CHUNK), cr_ref[p], cc_ref[p])
        total_re += jnp.where(keep, product[p * rows : (p + 1) * rows], 0.0)
        total_im += jnp.where(keep, product[half + p * rows : half + (p + 1) * rows], 0.0)
    for side in range(2):
        lanes = slice(side * LANES, (side + 1) * LANES)
        out_ref[0, side] = total_re[:, lanes].astype(BF16)
        out_ref[1, side] = total_im[:, lanes].astype(BF16)


def sum_kernel(in_ref, out_ref):
    total = in_ref[0].astype(F32)
    for i in range(1, in_ref.shape[0]):
        total += in_ref[i].astype(F32)
    total = total.astype(out_ref.dtype)
    for i in range(out_ref.shape[0]):
        out_ref[i] = total


def unpack_kernel(in_ref, re_ref, im_ref):
    for tile in range(8):
        lanes = slice(tile * LANES, (tile + 1) * LANES)
        re_ref[:, lanes] = in_ref[tile].astype(F32)
        im_ref[:, lanes] = in_ref[8 + tile].astype(F32)


def table_spec(band):
    return pl.BlockSpec((band, CHUNK), lambda n: (0, n))


def exchange(value, axis):
    return lax.all_to_all(value, axis, split_axis=0, concat_axis=0, tiled=True)


def sum_everywhere(value):
    received = exchange(value, "src")
    summed = pl.pallas_call(
        sum_kernel, out_shape=jax.ShapeDtypeStruct(value.shape, value.dtype), name="sum_parts"
    )(received)
    return exchange(summed, "src")


def local(spec_re, spec_im, target, weights, cent_row, cent_col):
    rows, band = spec_re.shape
    points = weights.shape[0]
    total_points = points * lax.axis_size("src")
    devices = lax.axis_size("row")
    wide = 2 * points * rows
    steps = band // CHUNK
    row = lax.axis_index("row").astype(jnp.int32).reshape(1)
    table = jax.ShapeDtypeStruct((band, band), BF16)
    parts = jax.ShapeDtypeStruct((devices, rows, wide), BF16)
    parts_spec = pl.BlockSpec((devices // steps, rows, wide), lambda n: (n, 0, 0))
    lhs = pltpu.VMEM((wide, 2 * band), BF16)

    cosine, sine, column_parts = pl.pallas_call(
        spectrum_kernel,
        grid=(steps,),
        in_specs=[SCALARS, SCALARS, SCALARS, pl.BlockSpec((64, CHUNK), lambda n: (0, n)), WHOLE, WHOLE],
        out_specs=[table_spec(band), table_spec(band), parts_spec],
        out_shape=[table, table, parts],
        scratch_shapes=[lhs],
        name="spectrum",
    )(row, cent_row, cent_col, trig_rows(band), spec_re, spec_im)
    columns = exchange(column_parts, "row").reshape(band, wide)
    field, power = pl.pallas_call(
        field_kernel,
        grid=(steps,),
        in_specs=[SCALARS, WHOLE, table_spec(band), table_spec(band)],
        out_specs=[
            pl.BlockSpec((wide, CHUNK), lambda n: (0, n)),
            pl.BlockSpec((4, 1, 16, LANES), lambda n: (0, n, 0, 0)),
        ],
        out_shape=[
            jax.ShapeDtypeStruct((wide, band), F32),
            jax.ShapeDtypeStruct((4, 4, 16, LANES), F32),
        ],
        scratch_shapes=[lhs],
        name="field",
    )(weights, columns, cosine, sine)
    power = sum_everywhere(power.reshape(16, 16, LANES)).reshape(4, 4, 16, LANES)
    adjoint_parts = pl.pallas_call(
        functools.partial(adjoint_kernel, total_points),
        grid=(steps,),
        in_specs=[SCALARS, WHOLE, WHOLE, WHOLE, table_spec(band), table_spec(band)],
        out_specs=parts_spec,
        out_shape=parts,
        scratch_shapes=[lhs],
        name="adjoint",
    )(weights, power, target, field, cosine, sine)
    adjoint = exchange(adjoint_parts, "row").reshape(band, wide)
    gradient = pl.pallas_call(
        gradient_kernel,
        grid=(steps,),
        in_specs=[SCALARS, SCALARS, SCALARS, WHOLE, table_spec(band), table_spec(band)],
        out_specs=pl.BlockSpec((2, 2, rows, LANES), lambda n: (0, n, 0, 0)),
        out_shape=jax.ShapeDtypeStruct((2, 8, rows, LANES), BF16),
        scratch_shapes=[lhs],
        name="gradient",
    )(row, cent_row, cent_col, adjoint, cosine, sine)
    gradient = sum_everywhere(gradient.reshape(16, rows, LANES))
    out = jax.ShapeDtypeStruct((rows, band), F32)
    return tuple(pl.pallas_call(unpack_kernel, out_shape=[out, out], name="unpack")(gradient))


def solution(mesh):
    return jax.shard_map(
        local,
        mesh=mesh,
        in_specs=(P("row", None), P("row", None), P("row", None), P("src"), P("src"), P("src")),
        out_specs=(P("row", None), P("row", None)),
        check_vma=False,
    )
```

time: 505 us -> 166 us (0.33)
  waiting for transfers between devices: 247 us -> 0 us
  local copies, waits for them, and re-layouts: 154 us -> 0 us
  blocking collectives: 0 us -> 132 us
  other arithmetic: 43.3 us -> 1.75 us
  Pallas kernels: 0 us -> 30.5 us
  between operations: 29.3 us -> 0.65 us
  matrix products: 20.2 us -> 0 us
  starting transfers between devices: 9.38 us -> 0 us
    psum x2 -> x0, waiting for transfers between devices: 234 us -> none  [the longest x1 117 us: local(): grad_re, grad_im = lax.psum((local_re, local_im), 'src')]
    all_to_all x0 -> x6, blocking collectives: none -> 132 us  [exchange(): return lax.all_to_all(value, axis, split_axis=0, concat_axis=0, tiled=True)]
    gather x96 -> x0, local copies, waits for them, and re-layouts: 97.7 us -> none
    convert_element_type x2 -> x0, other arithmetic: 31.6 us -> none  [the longest x1 15.8 us: make_tables(): (jnp.sin(angle) * factor).astype(jnp.bfloat16)]
    pallas_call x0 -> x7, Pallas kernels: none -> 30.5 us  [the longest x1 7.11 us: local(): pl.pallas_call(functools.partial(adjoint_kernel, total_points), grid=(ste...]
    unnamed x22 -> x0, local copies, waits for them, and re-layouts: 24.9 us -> none
    dot_general x4 -> x0, matrix products: 20.2 us -> none  [the longest x1 7.7 us: local(): jnp.einsum('pckl,plz->pckz', masked, narrow_windows, preferred_element_ty...]
    all_to_all x2 -> x0, local copies, waits for them, and re-layouts: 13.1 us -> none  [local(): lax.all_to_all(adjoint, 'row', split_axis=3, concat_axis=2, tiled=True)]
  transfers between devices with their start and end apart: 4 -> 0, of which waited for: 3 -> 0; matrix products, arithmetic and copies ran while one was open for 21% -> 0% of each run, Pallas kernels for 0% -> 0%
where the time goes in v1:
time: 166 us; the launch traced here: 165 us
  blocking collectives  132 us (80%)
  Pallas kernels  30.5 us (18%)
  other arithmetic  1.75 us (1%)
    all_to_all x6, blocking collectives, exchange(): return lax.all_to_all(value, axis, split_axis=0, concat_axis=0, tiled=True)  132 us
    pallas_call x1, Pallas kernels, local(): pl.pallas_call(functools.partial(adjoint_kernel, total_points), grid=(ste...  7.11 us
    pallas_call x1, Pallas kernels, local(): pl.pallas_call(field_kernel, grid=(steps,), in_specs=[SCALARS, WHOLE, tab...  6.61 us
    pallas_call x1, Pallas kernels, local(): pl.pallas_call(gradient_kernel, grid=(steps,), in_specs=[SCALARS, SCALARS...  6.17 us
    pallas_call x1, Pallas kernels, local(): pl.pallas_call(spectrum_kernel, grid=(steps,), in_specs=[SCALARS, SCALARS...  5.81 us

profile of v1, /device:TPU:1, one launch (start us, length us, event | category | flops | bytes accessed | tf_op | source)
XLA Modules:
  0.0 165.3 jit_solution(17848412202020602612)
XLA Ops:
  0.6 0.1 iota_multiply_fusion
  0.7 1.7 %fusion.3.trig_ref = f32[64,1024]{1,0:T(8,128)} fusion(s32[32,1024]{1,0:T(8,128)S(1)} %get-tuple-element.13, s32[32,1024]{1,0:T(8,128)S(1)} %get-tuple-element.12), kind=kLoop, calls=%fused_computation.6 | loop fusion | flops 917504 | bytes 524288 | tf_op jit(solution)/shard_map/cos | solution.py:26
  2.4 5.8 %spectrum.1 = (bf16[1024,1024]{1,0:T(8,128)(2,1)}, bf16[1024,1024]{1,0:T(8,128)(2,1)}, bf16[32,32,512]{2,1,0:T(8,128)(2,1)}) custom-call(s32[1]{0:T(128)} %bitcast.row_ref, s32[8]{0:T(128)} %cr_ref.3, s32[8]{0:T(128)} %cc_ref.3, f32[64,1024]{1,0:T(8,128)} %fusion.3.trig_ref, bf16[32,1024]{1,0:T(8,128)(2,1)} %re_ref.1, bf16[32,1024]{1,0:T(8,128)(2,1)} %im_ref.1), custom_call_target="tpu_custom_call" | custom-call | tf_op jit(solution)/shard_map/spectrum/pallas_call | solution.py:228
  8.2 35.2 %all_to_all.30 = bf16[32,32,512]{2,1,0:T(8,128)(2,1)} all-to-all(bf16[32,32,512]{2,1,0:T(8,128)(2,1)} %get-tuple-element.7), channel_id=1, replica_groups=mesh['src'=16,'row'=32] {'row'}, dimensions={0} | all-to-all | bytes 2097152 | tf_op jit(solution)/shard_map/all_to_all | solution.py:204
  43.5 6.6 %field.1 = (f32[512,1024]{1,0:T(8,128)}, f32[4,4,16,128]{3,2,1,0:T(8,128)}) custom-call(f32[8]{0:T(128)} %w_ref.3, bf16[1024,512]{1,0:T(8,128)(2,1)} %bitcast.6, bf16[1024,1024]{1,0:T(8,128)(2,1)} %get-tuple-element.8.cos_ref, bf16[1024,1024]{1,0:T(8,128)(2,1)} %get-tuple-element.9.sin_ref), custom_call_target="tpu_custom_call" | custom-call | tf_op jit(solution)/shard_map/field/pallas_call | solution.py:238
  50.1 24.3 %all_to_all.31.in_ref = f32[16,16,128]{2,1,0:T(8,128)} all-to-all(f32[16,16,128]{2,1,0:T(8,128)} %bitcast.10), channel_id=1, replica_groups=mesh['src'=16,'row'=32] {'src'}, dimensions={0} | all-to-all | bytes 262144 | tf_op jit(solution)/shard_map/all_to_all | solution.py:204
  74.3 1.6 sum_parts.2
  75.9 13.0 %all_to_all.32 = f32[16,16,128]{2,1,0:T(8,128)} all-to-all(f32[16,16,128]{2,1,0:T(8,128)} %sum_parts.2), channel_id=1, replica_groups=mesh['src'=16,'row'=32] {'src'}, dimensions={0} | all-to-all | bytes 262144 | tf_op jit(solution)/shard_map/all_to_all | solution.py:204
  89.0 7.1 %adjoint.1 = bf16[32,32,512]{2,1,0:T(8,128)(2,1)} custom-call(f32[8]{0:T(128)} %w_ref.3, f32[4,4,16,128]{3,2,1,0:T(8,128)} %bitcast.8, f32[32,1024]{1,0:T(8,128)} %target_ref.1, f32[512,1024]{1,0:T(8,128)} %get-tuple-element.11.field_ref, bf16[1024,1024]{1,0:T(8,128)(2,1)} %get-tuple-element.8.cos_ref, bf16[1024,1024]{1,0:T(8,128)(2,1)} %get-tuple-element.9.sin_ref), custom_call_target="tpu_custom_call" | custom-call | tf_op jit(solution)/shard_map/adjoint/pallas_call | solution.py:254
  96.1 32.0 %all_to_all.33 = bf16[32,32,512]{2,1,0:T(8,128)(2,1)} all-to-all(bf16[32,32,512]{2,1,0:T(8,128)(2,1)} %adjoint.1), channel_id=1, replica_groups=mesh['src'=16,'row'=32] {'row'}, dimensions={0} | all-to-all | bytes 2097152 | tf_op jit(solution)/shard_map/all_to_all | solution.py:204
  128.0 6.2 %gradient.1 = bf16[2,8,32,128]{3,2,1,0:T(8,128)(2,1)} custom-call(s32[1]{0:T(128)} %bitcast.row_ref, s32[8]{0:T(128)} %cr_ref.3, s32[8]{0:T(128)} %cc_ref.3, bf16[1024,512]{1,0:T(8,128)(2,1)} %bitcast.7, bf16[1024,1024]{1,0:T(8,128)(2,1)} %get-tuple-element.8.cos_ref, bf16[1024,1024]{1,0:T(8,128)(2,1)} %get-tuple-element.9.sin_ref), custom_call_target="tpu_custom_call" | custom-call | tf_op jit(solution)/shard_map/gradient/pallas_call | solution.py:264
  134.2 15.4 %all_to_all.34.in_ref = bf16[16,32,128]{2,1,0:T(8,128)(2,1)} all-to-all(bf16[16,32,128]{2,1,0:T(8,128)(2,1)} %bitcast.9), channel_id=1, replica_groups=mesh['src'=16,'row'=32] {'src'}, dimensions={0} | all-to-all | bytes 262144 | tf_op jit(solution)/shard_map/all_to_all | solution.py:204
  149.6 1.6 sum_parts.3
  151.1 12.5 %all_to_all.35.in_ref = bf16[16,32,128]{2,1,0:T(8,128)(2,1)} all-to-all(bf16[16,32,128]{2,1,0:T(8,128)(2,1)} %sum_parts.3), channel_id=1, replica_groups=mesh['src'=16,'row'=32] {'src'}, dimensions={0} | all-to-all | bytes 262144 | tf_op jit(solution)/shard_map/all_to_all | solution.py:204
  163.7 1.6 unpack.1
  (1 shorter events, 0.0 us)

commit v2 on v0

v2 whole, which is shorter than its diff:
```python
import math

import jax
import jax.numpy as jnp
from jax import lax
from jax.experimental import pallas as pl
from jax.experimental.pallas import tpu as pltpu
from jax.sharding import PartitionSpec as P

RAD = 128
F32 = jnp.float32
BF16 = jnp.bfloat16
CHUNK = 256
LANES = 128
STEPS = 4

WHOLE = pl.BlockSpec(memory_space=pltpu.VMEM)
SCALARS = pl.BlockSpec(memory_space=pltpu.SMEM)


def trig_rows(band):
    index = jnp.arange(64, dtype=jnp.int32)
    rows = jnp.where(index < 32, index, 32 * (index - 32))
    phase = rows[:, None] * jnp.arange(band, dtype=jnp.int32)[None, :]
    both = jnp.concatenate([phase, phase + (band - band // 4)], axis=0) % band
    return jnp.cos(both.astype(F32) * (2.0 * math.pi / band))


def dot_nt(left, right):
    return lax.dot_general(left, right, (((1,), (1,)), ((), ())), preferred_element_type=F32)


def dot_nn(left, right):
    return jnp.dot(left, right, preferred_element_type=F32)


def spectrum_kernel(row_ref, info_ref, trig_ref, re_ref, im_ref, cos_ref, sin_ref, out_ref, lhs_ref, flat_ref):
    step = pl.program_id(0)
    rows, band = re_ref.shape

    @pl.when(step == 0)
    def _():
        spec_re = re_ref[...].astype(F32)
        spec_im = im_ref[...].astype(F32)
        info = info_ref[0]
        centre_row, centre_col = info[:, 1:2], info[:, 2:3]
        col_gap = lax.broadcasted_iota(jnp.int32, (8, band), 1).astype(F32) - centre_col
        col_gap = col_gap * col_gap
        first = (row_ref[0] * rows).astype(F32)
        for k in range(rows):
            row_gap = first + float(k) - centre_row
            keep = row_gap * row_gap + col_gap <= float(RAD * RAD)
            part_re = jnp.where(keep, spec_re[k : k + 1, :], 0.0)
            part_im = jnp.where(keep, spec_im[k : k + 1, :], 0.0)
            place = slice(16 * k, 16 * k + 16)
            lhs_ref[place, :band] = jnp.concatenate([part_re, part_im], axis=0).astype(BF16)
            lhs_ref[place, band:] = jnp.concatenate([-part_im, part_re], axis=0).astype(BF16)

    scale = 1.0 / math.sqrt(band)
    base_c, base_s = trig_ref[0:32, :] * scale, trig_ref[64:96, :] * scale
    turn_c = trig_ref[pl.ds(pl.multiple_of(32 + 8 * step, 8), 8), :]
    turn_s = trig_ref[pl.ds(pl.multiple_of(96 + 8 * step, 8), 8), :]
    for r in range(8):
        c, s = turn_c[r : r + 1, :], turn_s[r : r + 1, :]
        cos_ref[32 * r : 32 * r + 32, :] = (c * base_c - s * base_s).astype(BF16)
        sin_ref[32 * r : 32 * r + 32, :] = (s * base_c + c * base_s).astype(BF16)
    product = dot_nt(cos_ref[...], lhs_ref[:, :band]) + dot_nt(sin_ref[...], lhs_ref[:, band:])
    for t in range(4):
        flat_ref[pl.ds(t, CHUNK, stride=4), :] = product[:, t * LANES : (t + 1) * LANES]
    low_row = lax.broadcasted_iota(jnp.int32, (8, LANES), 0) < 4
    low_lane = lax.broadcasted_iota(jnp.int32, (8, LANES), 1) < 64
    stay = low_row == low_lane
    for r in range(8):
        for s in range(16):
            first_row = 8 * (16 * r + s)
            tile = flat_ref[first_row : first_row + 8, :]
            moved = pltpu.roll(pltpu.roll(tile, 4, 0), 64, 1)
            out_ref[s, r] = jnp.where(stay, tile, moved).astype(BF16)


def tables_kernel(trig_ref, cos_k_ref, sin_k_ref, cos_y_ref, sin_y_ref):
    scale = 1.0 / math.sqrt(4 * trig_ref.shape[1])
    base_c, base_s = trig_ref[0:32, :] * scale, trig_ref[64:96, :] * scale
    turn_c, turn_s = trig_ref[32:64, :], trig_ref[96:128, :]
    for j in range(4):
        order = [j + 8 * (i % 4) + 4 * (i // 4) for i in range(8)]
        near_c = jnp.concatenate([base_c[f : f + 1, :] for f in order], axis=0)
        near_s = jnp.concatenate([base_s[f : f + 1, :] for f in order], axis=0)
        for r in range(0, 32, 2):
            cs, ss = [], []
            for turn in (r, r + 1):
                c, s = turn_c[turn : turn + 1, :], turn_s[turn : turn + 1, :]
                cs.append(c * near_c - s * near_s)
                ss.append(s * near_c + c * near_s)
            place = slice(256 * j + 8 * r, 256 * j + 8 * r + 16)
            cos_k_ref[place, :] = jnp.concatenate(cs, axis=0).astype(BF16)
            sin_k_ref[place, :] = jnp.concatenate(ss, axis=0).astype(BF16)
    for f in range(32):
        c, s = base_c[f : f + 1, :], base_s[f : f + 1, :]
        first = 512 * (f % 2) + 32 * (f // 2)
        cos_y_ref[first : first + 32, :] = (c * turn_c - s * turn_s).astype(BF16)
        sin_y_ref[first : first + 32, :] = (s * turn_c + c * turn_s).astype(BF16)


def image_kernel(
    src_ref, info_ref, in_ref, target_ref, cos_k_ref, sin_k_ref, cos_ref, sin_ref, out_ref, lhs_ref, grad_ref, flat_ref
):
    step = pl.program_id(0)

    @pl.when(step == 0)
    def _():
        for s in range(16):
            turned = in_ref[256 * s : 256 * s + 256, :].T
            for y in range(2):
                for j in range(4):
                    lhs_ref[32 * s + 16 * y : 32 * s + 16 * y + 16, 256 * j : 256 * j + 256] = turned[
                        64 * y + 16 * j : 64 * y + 16 * j + 16
                    ]

    @pl.when(step < STEPS)
    def _():
        by_cos = dot_nn(lhs_ref[...], cos_k_ref[...])
        by_sin = dot_nn(lhs_ref[...], sin_k_ref[...])

        def field(s, y):
            at = 32 * s + 16 * y
            re = by_cos[at : at + 8] - by_sin[at + 8 : at + 16]
            im = by_sin[at : at + 8] + by_cos[at + 8 : at + 16]
            return re, im

        for y in range(2):
            power = jnp.zeros((8, CHUNK), F32)
            for s in range(16):
                re, im = field(s, y)
                power += info_ref[s, :, 0:1] * (re * re + im * im)
            intensity = jnp.sum(power, axis=0, keepdims=True) * (1.0 / 128.0)
            mismatch = intensity - target_ref[pl.ds(2 * src_ref[0] + y, 1), :]
            for s in range(0, 16, 2):
                grads_re, grads_im = [], []
                for one in (s, s + 1):
                    re, im = field(one, y)
                    factor = (2.0 * info_ref[one, :, 0:1]) * mismatch
                    grads_re.append(factor * re)
                    grads_im.append(factor * im)
                at = 256 * y + 8 * s
                grad_ref[step, at : at + 16, :] = jnp.concatenate(grads_re, axis=0).astype(BF16)
                grad_ref[step, at + 128 : at + 144, :] = jnp.concatenate(grads_im, axis=0).astype(BF16)

    @pl.when(step >= STEPS)
    def _():
        by_cos = jnp.zeros((CHUNK, 512), F32)
        by_sin = jnp.zeros((CHUNK, 512), F32)
        for n in range(STEPS):
            cols = slice(n * CHUNK, (n + 1) * CHUNK)
            by_cos += dot_nt(cos_ref[:, cols], grad_ref[n])
            by_sin += dot_nt(sin_ref[:, cols], grad_ref[n])
        for y in range(2):
            re, im = slice(256 * y, 256 * y + 128), slice(256 * y + 128, 256 * y + 256)
            flat_ref[pl.ds(2 * y, CHUNK, stride=4), :] = by_cos[:, re] + by_sin[:, im]
            flat_ref[pl.ds(2 * y + 1, CHUNK, stride=4), :] = by_cos[:, im] - by_sin[:, re]
        for r in range(8):
            for s in range(16):
                first_row = 8 * (16 * r + s)
                out_ref[s, r] = flat_ref[first_row : first_row + 8, :].astype(BF16)


def gradient_kernel(place_ref, info_ref, in_ref, cos_ref, sin_ref, out_ref, lhs_ref, flat_ref, sums_ref):
    step = pl.program_id(0)

    @pl.when(step == 0)
    def _():
        for first in range(0, 4096, 512):
            flat_ref[first : first + 512, :] = in_ref[first : first + 512, :].astype(F32)
        for k in range(2):
            for y in range(2):
                for c in range(2):
                    part = flat_ref[pl.ds(4 * k + 2 * y + c, 512, stride=8), :]
                    lhs_ref[128 * (2 * c + k) : 128 * (2 * c + k) + 128, 512 * y : 512 * y + 512] = part.T.astype(BF16)

    by_cos = dot_nn(lhs_ref[...], cos_ref[...])
    by_sin = dot_nn(lhs_ref[...], sin_ref[...])
    centre_row, centre_col = info_ref[:, 1:2], info_ref[:, 2:3]
    first_col = (step * CHUNK).astype(F32)
    col_gap = lax.broadcasted_iota(jnp.int32, (LANES, CHUNK), 1).astype(F32) + (first_col - centre_col)
    col_gap = col_gap * col_gap
    for k in range(2):
        row_gap = (place_ref[0] + k).astype(F32) - centre_row
        keep = row_gap * row_gap + col_gap <= float(RAD * RAD)
        re, im = slice(128 * k, 128 * k + 128), slice(256 + 128 * k, 256 + 128 * k + 128)
        terms = (by_cos[re] + by_sin[im], by_cos[im] - by_sin[re])
        for c in range(2):
            total = jnp.sum(jnp.where(keep, terms[c], 0.0), axis=0, keepdims=True)
            for side in range(2):
                sums_ref[pl.ds(16 * k + 8 * c + 2 * step + side, 1), :] = total[:, side * LANES : (side + 1) * LANES]

    @pl.when(step == STEPS - 1)
    def _():
        for i in range(16):
            out_ref[i] = sums_ref[...].astype(BF16)


def unpack_kernel(in_ref, re_ref, im_ref, flat_ref):
    flat_ref[...] = in_ref[...].astype(F32)
    for c, ref in enumerate((re_ref, im_ref)):
        for tile in range(8):
            ref[:, tile * LANES : (tile + 1) * LANES] = flat_ref[pl.ds(8 * c + tile, 32, stride=16), :]


def exchange(value, axis):
    return lax.all_to_all(value, axis, split_axis=0, concat_axis=0, tiled=True)


def local(spec_re, spec_im, target, weights, cent_row, cent_col):
    rows, band = spec_re.shape
    everyone = ("src", "row")
    row = lax.axis_index("row").astype(jnp.int32).reshape(1)
    src = lax.axis_index("src").astype(jnp.int32).reshape(1)
    lane = lax.broadcasted_iota(jnp.int32, (16, 8, LANES), 2)
    info = jnp.where(lane == 1, cent_row.astype(F32)[None, :, None], cent_col.astype(F32)[None, :, None])
    info = jnp.where(lane == 0, weights[None, :, None], info)
    trig = trig_rows(band)
    table = jax.ShapeDtypeStruct((band, band), BF16)
    parts = jax.ShapeDtypeStruct((16, 32, 8, LANES), BF16)
    row_block = pl.BlockSpec((CHUNK, band), lambda n: (n, 0))
    col_block = pl.BlockSpec((band, CHUNK), lambda n: (0, n))

    all_info = exchange(info, "src")
    cosine, sine, column_parts = pl.pallas_call(
        spectrum_kernel,
        grid=(STEPS,),
        in_specs=[SCALARS, WHOLE, WHOLE, WHOLE, WHOLE],
        out_specs=[row_block, row_block, pl.BlockSpec((16, 8, 8, LANES), lambda n: (0, n, 0, 0))],
        out_shape=[table, table, parts],
        scratch_shapes=[pltpu.VMEM((512, 2 * band), BF16), pltpu.VMEM((4 * CHUNK, LANES), F32)],
        name="spectrum",
    )(row, info, trig, spec_re, spec_im)
    cos_k, sin_k, cos_y, sin_y = pl.pallas_call(
        tables_kernel,
        grid=(STEPS,),
        in_specs=[pl.BlockSpec((128, CHUNK), lambda n: (0, n))],
        out_specs=[col_block] * 4,
        out_shape=[table] * 4,
        cost_estimate=pl.CostEstimate(flops=12 * band * band, bytes_accessed=8 * band * band, transcendentals=0),
        name="tables",
    )(trig)
    columns = exchange(column_parts.reshape(512, 8, LANES), everyone).reshape(4096, LANES)
    adjoint_parts = pl.pallas_call(
        image_kernel,
        grid=(2 * STEPS,),
        in_specs=[
            SCALARS,
            WHOLE,
            WHOLE,
            pl.BlockSpec((rows, CHUNK), lambda n: (0, jnp.minimum(n, STEPS - 1))),
            pl.BlockSpec((band, CHUNK), lambda n: (0, jnp.minimum(n, STEPS - 1))),
            pl.BlockSpec((band, CHUNK), lambda n: (0, jnp.minimum(n, STEPS - 1))),
            pl.BlockSpec((CHUNK, band), lambda n: (jnp.maximum(n - STEPS, 0), 0)),
            pl.BlockSpec((CHUNK, band), lambda n: (jnp.maximum(n - STEPS, 0), 0)),
        ],
        out_specs=pl.BlockSpec((16, 8, 8, LANES), lambda n: (0, jnp.maximum(n - STEPS, 0), 0, 0)),
        out_shape=parts,
        scratch_shapes=[
            pltpu.VMEM((512, band), BF16),
            pltpu.VMEM((STEPS, 512, CHUNK), BF16),
            pltpu.VMEM((4 * CHUNK, LANES), F32),
        ],
        name="image",
    )(src, all_info, columns, target, cos_k, sin_k, cosine, sine)
    adjoint = exchange(adjoint_parts.reshape(512, 8, LANES), everyone).reshape(4096, LANES)
    gradient = pl.pallas_call(
        gradient_kernel,
        grid=(STEPS,),
        in_specs=[SCALARS, WHOLE, WHOLE, col_block, col_block],
        out_specs=WHOLE,
        out_shape=jax.ShapeDtypeStruct((16, 32, LANES), BF16),
        scratch_shapes=[
            pltpu.VMEM((512, band), BF16),
            pltpu.VMEM((4096, LANES), F32),
            pltpu.VMEM((32, LANES), F32),
        ],
        name="gradient",
    )(row * rows + 2 * src, all_info.reshape(LANES, LANES), adjoint, cos_y, sin_y)
    gradient = exchange(gradient, "src").reshape(512, LANES)
    out = jax.ShapeDtypeStruct((rows, band), F32)
    return tuple(
        pl.pallas_call(
            unpack_kernel, out_shape=[out, out], scratch_shapes=[pltpu.VMEM((512, LANES), F32)], name="unpack"
        )(gradient)
    )


def solution(mesh):
    return jax.shard_map(
        local,
        mesh=mesh,
        in_specs=(P("row", None), P("row", None), P("row", None), P("src"), P("src"), P("src")),
        out_specs=(P("row", None), P("row", None)),
        check_vma=False,
    )
```

time: 505 us -> 152 us (0.30)
  waiting for transfers between devices: 247 us -> 60.8 us
  local copies, waits for them, and re-layouts: 154 us -> 1.94 us
  other arithmetic: 43.3 us -> 5.42 us
  Pallas kernels: 0 us -> 30 us
  starting transfers between devices: 9.38 us -> 38.3 us
  between operations: 29.3 us -> 0.68 us
  matrix products: 20.2 us -> 0 us
  blocking collectives: 0 us -> 13.9 us
    psum x2 -> x0, waiting for transfers between devices: 234 us -> none  [the longest x1 117 us: local(): grad_re, grad_im = lax.psum((local_re, local_im), 'src')]
    gather x96 -> x0, local copies, waits for them, and re-layouts: 97.7 us -> none
    all_to_all x1 -> x3, waiting for transfers between devices: 0.01 us -> 60.8 us  [exchange(): return lax.all_to_all(value, axis, split_axis=0, concat_axis=0, tiled=True)]
    convert_element_type x2, other arithmetic: 31.6 us -> 1.32 us  [the longest x1 0.66 us: local(): cent_row.astype(F32)[None, :, None]]
    pallas_call x0 -> x5, Pallas kernels: none -> 30 us  [the longest x1 11 us: local(): pl.pallas_call(image_kernel, grid=(2 * STEPS,), in_specs=[SCALARS, WHOLE,...]
    all_to_all x1 -> x3, starting transfers between devices: 9.26 us -> 38.3 us  [exchange(): return lax.all_to_all(value, axis, split_axis=0, concat_axis=0, tiled=True)]
    unnamed x22 -> x6, local copies, waits for them, and re-layouts: 24.9 us -> 1.94 us
    dot_general x4 -> x0, matrix products: 20.2 us -> none  [the longest x1 7.7 us: local(): jnp.einsum('pckl,plz->pckz', masked, narrow_windows, preferred_element_ty...]
  transfers between devices with their start and end apart: 4 -> 3, of which waited for: 3 -> 2; matrix products, arithmetic and copies ran while one was open for 21% -> 2% of each run, Pallas kernels for 0% -> 7%
where the time goes in v2:
time: 152 us; the launch traced here: 151 us
  waiting for transfers between devices  60.8 us (40%)
  starting transfers between devices  38.3 us (25%)
  Pallas kernels  30 us (20%)
  blocking collectives  13.9 us (9%)
  other arithmetic  5.42 us (4%)
  local copies, waits for them, and re-layouts  1.94 us (1%)
    all_to_all x3, waiting for transfers between devices, exchange(): return lax.all_to_all(value, axis, split_axis=0, concat_axis=0, tiled=True)  60.8 us
    all_to_all x3, starting transfers between devices, exchange(): return lax.all_to_all(value, axis, split_axis=0, concat_axis=0, tiled=True)  38.3 us
    all_to_all x1, blocking collectives, exchange(): return lax.all_to_all(value, axis, split_axis=0, concat_axis=0, tiled=True)  13.9 us
    pallas_call x1, Pallas kernels, local(): pl.pallas_call(image_kernel, grid=(2 * STEPS,), in_specs=[SCALARS, WHOLE,...  11 us
    pallas_call x1, Pallas kernels, local(): pl.pallas_call(gradient_kernel, grid=(STEPS,), in_specs=[SCALARS, WHOLE,...  6.37 us
    pallas_call x1, Pallas kernels, local(): pl.pallas_call(spectrum_kernel, grid=(STEPS,), in_specs=[SCALARS, WHOLE,...  5.76 us
    pallas_call x1, Pallas kernels, local(): pl.pallas_call(tables_kernel, grid=(STEPS,), in_specs=[pl.BlockSpec((128,...  5.15 us
  transfers between devices with their start and end apart: 3, of which 2 were waited for; matrix products, arithmetic and copies ran while one was open for 2% of the time, Pallas kernels for 7%

profile of v2, /device:TPU:1, one launch (start us, length us, event | category | flops | bytes accessed | tf_op | source)
XLA Modules:
  0.0 151.0 jit_solution(5468844614551672887)
XLA Ops:
  0.6 0.7 convert_element_type.9
  1.3 0.7 convert_element_type.10
  2.0 1.4 select_select_fusion.info_ref
  3.3 11.8 %all-to-all-start = ((f32[16,8,128]{2,1,0:T(8,128)}), f32[16,8,128]{2,1,0:T(8,128)S(1)}, u32[]{:S(2)}, u32[]{:S(2)}) async-start(f32[16,8,128]{2,1,0:T(8,128)} %select_select_fusion.info_ref), calls=%async_computation | async-start | bytes 131072 | tf_op jit(solution)/shard_map/all_to_all | solution.py:210
  15.1 0.1 iota_multiply_fusion
  15.3 2.6 %fusion.3.trig_ref = f32[128,1024]{1,0:T(8,128)} fusion(s32[64,1024]{1,0:T(8,128)S(1)} %get-tuple-element.17, s32[64,1024]{1,0:T(8,128)S(1)} %get-tuple-element.16), kind=kLoop, calls=%fused_computation.6 | loop fusion | flops 1835008 | bytes 1048576 | tf_op jit(solution)/shard_map/cos | solution.py:26
  17.9 5.8 %spectrum.1 = (bf16[1024,1024]{1,0:T(8,128)(2,1)}, bf16[1024,1024]{1,0:T(8,128)(2,1)}, bf16[16,32,8,128]{3,2,1,0:T(8,128)(2,1)}) custom-call(s32[1]{0:T(128)} %bitcast.row_ref, f32[16,8,128]{2,1,0:T(8,128)} %select_select_fusion.info_ref, f32[128,1024]{1,0:T(8,128)} %fusion.3.trig_ref, bf16[32,1024]{1,0:T(8,128)(2,1)} %re_ref.1, bf16[32,1024]{1,0:T(8,128)(2,1)} %im_ref.1), custom_call_target="tpu_custom_call" | custom-call | tf_op jit(solution)/shard_map/spectrum/pallas_call | solution.py:228
  23.6 0.0 all-to-all-done.info_ref
  23.7 0.0 copy-start.2
  23.7 17.6 %all-to-all-start.1 = ((bf16[512,8,128]{2,1,0:T(8,128)(2,1)}), bf16[512,8,128]{2,1,0:T(8,128)(2,1)S(1)}, u32[]{:S(2)}, u32[]{:S(2)}) async-start(bf16[512,8,128]{2,1,0:T(8,128)(2,1)} %bitcast.11), calls=%async_computation.1 | async-start | bytes 2097152 | tf_op jit(solution)/shard_map/all_to_all | solution.py:210
  41.2 5.1 %tables.1 = (bf16[1024,1024]{1,0:T(8,128)(2,1)}, bf16[1024,1024]{1,0:T(8,128)(2,1)}, bf16[1024,1024]{1,0:T(8,128)(2,1)}, bf16[1024,1024]{1,0:T(8,128)(2,1)}) custom-call(f32[128,1024]{1,0:T(8,128)} %fusion.3.trig_ref), custom_call_target="tpu_custom_call" | custom-call | flops 12582912 | bytes 8388608 | tf_op jit(solution)/shard_map/tables/pallas_call | solution.py:237
  46.4 27.7 %all-to-all-done.1 = bf16[512,8,128]{2,1,0:T(8,128)(2,1)S(1)} async-done(((bf16[512,8,128]{2,1,0:T(8,128)(2,1)}), bf16[512,8,128]{2,1,0:T(8,128)(2,1)S(1)}, u32[]{:S(2)}, u32[]{:S(2)}) %all-to-all-start.1) | async-done | bytes 1048608 | tf_op jit(solution)/shard_map/all_to_all | solution.py:210
  74.1 0.0 copy-start.1
  74.1 0.0 copy-done.2
  74.1 1.0 copy-done.1
  75.1 11.0 %image.1 = bf16[16,32,8,128]{3,2,1,0:T(8,128)(2,1)} custom-call(s32[1]{0:T(128)} %bitcast.1.src_ref, f32[16,8,128]{2,1,0:T(8,128)} %copy-done.2, bf16[4096,128]{1,0:T(8,128)(2,1)} %bitcast.9, f32[32,1024]{1,0:T(8,128)} %target_ref.1, bf16[1024,1024]{1,0:T(8,128)(2,1)} %get-tuple-element.10.cos_k_ref, bf16[1024,1024]{1,0:T(8,128)(2,1)} %get-tuple-element.11.sin_k_ref, ...), custom_call_target="tpu_custom_call" | custom-call | tf_op jit(solution)/shard_map/image/pallas_call | solution.py:247
  86.1 9.0 %all-to-all-start.2 = ((bf16[512,8,128]{2,1,0:T(8,128)(2,1)}), bf16[512,8,128]{2,1,0:T(8,128)(2,1)S(1)}, u32[]{:S(2)}, u32[]{:S(2)}) async-start(bf16[512,8,128]{2,1,0:T(8,128)(2,1)} %bitcast.10), calls=%async_computation.2 | async-start | bytes 2097152 | tf_op jit(solution)/shard_map/all_to_all | solution.py:210
  95.1 33.0 %all-to-all-done.2 = bf16[512,8,128]{2,1,0:T(8,128)(2,1)S(1)} async-done(((bf16[512,8,128]{2,1,0:T(8,128)(2,1)}), bf16[512,8,128]{2,1,0:T(8,128)(2,1)S(1)}, u32[]{:S(2)}, u32[]{:S(2)}) %all-to-all-start.2) | async-done | bytes 1048608 | tf_op jit(solution)/shard_map/all_to_all | solution.py:210
  128.1 0.0 copy-start
  128.1 1.0 copy-done
  129.1 6.4 %gradient.1 = bf16[16,32,128]{2,1,0:T(8,128)(2,1)} custom-call(s32[1]{0:T(128)S(6)} %add.20.place_ref, f32[128,128]{1,0:T(8,128)} %bitcast.12, bf16[4096,128]{1,0:T(8,128)(2,1)} %bitcast.8, bf16[1024,1024]{1,0:T(8,128)(2,1)} %get-tuple-element.14.cos_ref, bf16[1024,1024]{1,0:T(8,128)(2,1)} %get-tuple-element.15.sin_ref), custom_call_target="tpu_custom_call" | custom-call | tf_op jit(solution)/shard_map/gradient/pallas_call | solution.py:270
  135.4 13.9 %all_to_all.20 = bf16[16,32,128]{2,1,0:T(8,128)(2,1)} all-to-all(bf16[16,32,128]{2,1,0:T(8,128)(2,1)} %gradient.1), channel_id=1, replica_groups=mesh['src'=16,'row'=32] {'src'}, dimensions={0} | all-to-all | bytes 262144 | tf_op jit(solution)/shard_map/all_to_all | solution.py:210
  149.3 1.7 %unpack.1 = (f32[32,1024]{1,0:T(8,128)}, f32[32,1024]{1,0:T(8,128)}) custom-call(bf16[512,128]{1,0:T(8,128)(2,1)} %bitcast.13), custom_call_target="tpu_custom_call" | custom-call | tf_op jit(solution)/shard_map/unpack/pallas_call | solution.py:286
  (2 shorter events, 0.0 us)
Async XLA Ops:
  3.3 20.3 %all-to-all-start = ((f32[16,8,128]{2,1,0:T(8,128)}), f32[16,8,128]{2,1,0:T(8,128)S(1)}, u32[]{:S(2)}, u32[]{:S(2)}) async-start(f32[16,8,128]{2,1,0:T(8,128)} %select_select_fusion.info_ref), calls=%async_computation | async-start | bytes 131072 | tf_op jit(solution)/shard_map/all_to_all | solution.py:210
  23.7 50.5 %copy-start.2 = (f32[16,8,128]{2,1,0:T(8,128)}, f32[16,8,128]{2,1,0:T(8,128)S(1)}, u32[]{:S(2)}) copy-start(f32[16,8,128]{2,1,0:T(8,128)S(1)} %all-to-all-done.info_ref) | copy-start | bytes 196612
  23.7 50.5 %all-to-all-start.1 = ((bf16[512,8,128]{2,1,0:T(8,128)(2,1)}), bf16[512,8,128]{2,1,0:T(8,128)(2,1)S(1)}, u32[]{:S(2)}, u32[]{:S(2)}) async-start(bf16[512,8,128]{2,1,0:T(8,128)(2,1)} %bitcast.11), calls=%async_computation.1 | async-start | bytes 2097152 | tf_op jit(solution)/shard_map/all_to_all | solution.py:210
  74.1 1.0 copy-start.1
  86.1 42.0 %all-to-all-start.2 = ((bf16[512,8,128]{2,1,0:T(8,128)(2,1)}), bf16[512,8,128]{2,1,0:T(8,128)(2,1)S(1)}, u32[]{:S(2)}, u32[]{:S(2)}) async-start(bf16[512,8,128]{2,1,0:T(8,128)(2,1)} %bitcast.10), calls=%async_computation.2 | async-start | bytes 2097152 | tf_op jit(solution)/shard_map/all_to_all | solution.py:210
  128.1 1.0 copy-start

commit v3 on v2

--- a/solution.py
+++ b/solution.py
@@ -7,10 +7,12 @@
 from jax.experimental.pallas import tpu as pltpu
 from jax.sharding import PartitionSpec as P
 
+
 RAD = 128
 F32 = jnp.float32
 BF16 = jnp.bfloat16
 CHUNK = 256
+WIDE = 512
 LANES = 128
 STEPS = 4
 
@@ -19,13 +21,39 @@
 
 
 def trig_rows(band):
-    index = jnp.arange(64, dtype=jnp.int32)
-    rows = jnp.where(index < 32, index, 32 * (index - 32))
+    index = jnp.arange(24, dtype=jnp.int32)
+    rows = jnp.where(index < 8, index, 128 * (index - 8))
+    rows = jnp.where(index < 16, rows, jnp.where(index < 20, 8 * (index - 16), 32 * (index - 20)))
     phase = rows[:, None] * jnp.arange(band, dtype=jnp.int32)[None, :]
     both = jnp.concatenate([phase, phase + (band - band // 4)], axis=0) % band
     return jnp.cos(both.astype(F32) * (2.0 * math.pi / band))
 
 
+def rotate(one, other):
+    return one[0] * other[0] - one[1] * other[1], one[1] * other[0] + one[0] * other[1]
+
+
+def pick(trig, first, count=1):
+    return trig[first : first + count, :], trig[24 + first : 24 + first + count, :]
+
+
+def base_rows(trig, scale):
+    fine = tuple(part * scale for part in pick(trig, 0, 8))
+    blocks = [rotate(pick(trig, 16 + b), fine) for b in range(4)]
+    return tuple(jnp.concatenate([block[i] for block in blocks], axis=0) for i in range(2))
+
+
+def info_tile(w_ref, cr_ref, cc_ref):
+    shape = (8, LANES)
+    sublane = lax.broadcasted_iota(jnp.int32, shape, 0)
+    lane = lax.broadcasted_iota(jnp.int32, shape, 1)
+    tile = jnp.zeros(shape, F32)
+    for p in range(8):
+        centre = jnp.where(lane == 1, cr_ref[p].astype(F32), cc_ref[p].astype(F32))
+        tile = jnp.where(sublane == p, jnp.where(lane == 0, w_ref[p], centre), tile)
+    return tile
+
+
 def dot_nt(left, right):
     return lax.dot_general(left, right, (((1,), (1,)), ((), ())), preferred_element_type=F32)
 
@@ -34,7 +62,7 @@
     return jnp.dot(left, right, preferred_element_type=F32)
 
 
-def spectrum_kernel(row_ref, info_ref, trig_ref, re_ref, im_ref, cos_ref, sin_ref, out_ref, lhs_ref, flat_ref):
+def spectrum_kernel(row_ref, w_ref, cr_ref, cc_ref, trig_ref, re_ref, im_ref, out_ref, lhs_ref, cos_ref, sin_ref, flat_ref):
     step = pl.program_id(0)
     rows, band = re_ref.shape
 
@@ -42,7 +70,7 @@
     def _():
         spec_re = re_ref[...].astype(F32)
         spec_im = im_ref[...].astype(F32)
-        info = info_ref[0]
+        info = info_tile(w_ref, cr_ref, cc_ref)
         centre_row, centre_col = info[:, 1:2], info[:, 2:3]
         col_gap = lax.broadcasted_iota(jnp.int32, (8, band), 1).astype(F32) - centre_col
         col_gap = col_gap * col_gap
@@ -56,21 +84,21 @@
             lhs_ref[place, :band] = jnp.concatenate([part_re, part_im], axis=0).astype(BF16)
             lhs_ref[place, band:] = jnp.concatenate([-part_im, part_re], axis=0).astype(BF16)
 
-    scale = 1.0 / math.sqrt(band)
-    base_c, base_s = trig_ref[0:32, :] * scale, trig_ref[64:96, :] * scale
-    turn_c = trig_ref[pl.ds(pl.multiple_of(32 + 8 * step, 8), 8), :]
-    turn_s = trig_ref[pl.ds(pl.multiple_of(96 + 8 * step, 8), 8), :]
-    for r in range(8):
-        c, s = turn_c[r : r + 1, :], turn_s[r : r + 1, :]
-        cos_ref[32 * r : 32 * r + 32, :] = (c * base_c - s * base_s).astype(BF16)
-        sin_ref[32 * r : 32 * r + 32, :] = (s * base_c + c * base_s).astype(BF16)
+    base = base_rows(trig_ref, 1.0 / math.sqrt(band))
+    for a in range(4):
+        coarse = tuple(trig_ref[pl.ds(first + 4 * step + a, 1), :] for first in (8, 32))
+        for d in range(4):
+            cos, sin = rotate(rotate(coarse, pick(trig_ref, 20 + d)), base)
+            place = slice(128 * a + 32 * d, 128 * a + 32 * d + 32)
+            cos_ref[place, :] = cos.astype(BF16)
+            sin_ref[place, :] = sin.astype(BF16)
     product = dot_nt(cos_ref[...], lhs_ref[:, :band]) + dot_nt(sin_ref[...], lhs_ref[:, band:])
     for t in range(4):
-        flat_ref[pl.ds(t, CHUNK, stride=4), :] = product[:, t * LANES : (t + 1) * LANES]
+        flat_ref[pl.ds(t, WIDE, stride=4), :] = product[:, t * LANES : (t + 1) * LANES]
     low_row = lax.broadcasted_iota(jnp.int32, (8, LANES), 0) < 4
     low_lane = lax.broadcasted_iota(jnp.int32, (8, LANES), 1) < 64
     stay = low_row == low_lane
-    for r in range(8):
+    for r in range(16):
         for s in range(16):
             first_row = 8 * (16 * r + s)
             tile = flat_ref[first_row : first_row + 8, :]
@@ -78,10 +106,20 @@
             out_ref[s, r] = jnp.where(stay, tile, moved).astype(BF16)
 
 
-def tables_kernel(trig_ref, cos_k_ref, sin_k_ref, cos_y_ref, sin_y_ref):
-    scale = 1.0 / math.sqrt(4 * trig_ref.shape[1])
-    base_c, base_s = trig_ref[0:32, :] * scale, trig_ref[64:96, :] * scale
-    turn_c, turn_s = trig_ref[32:64, :], trig_ref[96:128, :]
+def tables_kernel(
+    w_ref, cr_ref, cc_ref, trig_ref, _, info_ref, cos_ref, sin_ref, cos_k_ref, sin_k_ref, cos_y_ref, sin_y_ref
+):
+    @pl.when(pl.program_id(0) == 0)
+    def _():
+        info_ref[0] = info_tile(w_ref, cr_ref, cc_ref)
+
+    base_c, base_s = base_rows(trig_ref, 1.0 / math.sqrt(4 * trig_ref.shape[1]))
+    turns = [rotate(pick(trig_ref, 8 + a), pick(trig_ref, 20 + d)) for a in range(8) for d in range(4)]
+    turn_c, turn_s = (jnp.concatenate([turn[i] for turn in turns], axis=0) for i in range(2))
+    for r in range(32):
+        cos, sin = rotate(turns[r], (base_c, base_s))
+        cos_ref[32 * r : 32 * r + 32, :] = cos.astype(BF16)
+        sin_ref[32 * r : 32 * r + 32, :] = sin.astype(BF16)
     for j in range(4):
         order = [j + 8 * (i % 4) + 4 * (i // 4) for i in range(8)]
         near_c = jnp.concatenate([base_c[f : f + 1, :] for f in order], axis=0)
@@ -107,6 +145,9 @@
 ):
     step = pl.program_id(0)
 
+    def weight(s):
+        return info_ref[jnp.bitwise_xor(src_ref[0], s)][:, 0:1]
+
     @pl.when(step == 0)
     def _():
         for s in range(16):
@@ -132,14 +173,14 @@
             power = jnp.zeros((8, CHUNK), F32)
             for s in range(16):
                 re, im = field(s, y)
-                power += info_ref[s, :, 0:1] * (re * re + im * im)
+                power += weight(s) * (re * re + im * im)
             intensity = jnp.sum(power, axis=0, keepdims=True) * (1.0 / 128.0)
             mismatch = intensity - target_ref[pl.ds(2 * src_ref[0] + y, 1), :]
             for s in range(0, 16, 2):
                 grads_re, grads_im = [], []
                 for one in (s, s + 1):
                     re, im = field(one, y)
-                    factor = (2.0 * info_ref[one, :, 0:1]) * mismatch
+                    factor = (2.0 * weight(one)) * mismatch
                     grads_re.append(factor * re)
                     grads_im.append(factor * im)
                 at = 256 * y + 8 * s
@@ -148,23 +189,23 @@
 
     @pl.when(step >= STEPS)
     def _():
-        by_cos = jnp.zeros((CHUNK, 512), F32)
-        by_sin = jnp.zeros((CHUNK, 512), F32)
+        by_cos = jnp.zeros((WIDE, 512), F32)
+        by_sin = jnp.zeros((WIDE, 512), F32)
         for n in range(STEPS):
             cols = slice(n * CHUNK, (n + 1) * CHUNK)
             by_cos += dot_nt(cos_ref[:, cols], grad_ref[n])
             by_sin += dot_nt(sin_ref[:, cols], grad_ref[n])
         for y in range(2):
             re, im = slice(256 * y, 256 * y + 128), slice(256 * y + 128, 256 * y + 256)
-            flat_ref[pl.ds(2 * y, CHUNK, stride=4), :] = by_cos[:, re] + by_sin[:, im]
-            flat_ref[pl.ds(2 * y + 1, CHUNK, stride=4), :] = by_cos[:, im] - by_sin[:, re]
-        for r in range(8):
+            flat_ref[pl.ds(2 * y, WIDE, stride=4), :] = by_cos[:, re] + by_sin[:, im]
+            flat_ref[pl.ds(2 * y + 1, WIDE, stride=4), :] = by_cos[:, im] - by_sin[:, re]
+        for r in range(16):
             for s in range(16):
                 first_row = 8 * (16 * r + s)
                 out_ref[s, r] = flat_ref[first_row : first_row + 8, :].astype(BF16)
 
 
-def gradient_kernel(place_ref, info_ref, in_ref, cos_ref, sin_ref, out_ref, lhs_ref, flat_ref, sums_ref):
+def gradient_kernel(place_ref, src_ref, info_ref, in_ref, cos_ref, sin_ref, out_ref, lhs_ref, flat_ref, sums_ref):
     step = pl.program_id(0)
 
     @pl.when(step == 0)
@@ -179,7 +220,8 @@
 
     by_cos = dot_nn(lhs_ref[...], cos_ref[...])
     by_sin = dot_nn(lhs_ref[...], sin_ref[...])
-    centre_row, centre_col = info_ref[:, 1:2], info_ref[:, 2:3]
+    info = jnp.concatenate([info_ref[jnp.bitwise_xor(src_ref[0], s)] for s in range(16)], axis=0)
+    centre_row, centre_col = info[:, 1:2], info[:, 2:3]
     first_col = (step * CHUNK).astype(F32)
     col_gap = lax.broadcasted_iota(jnp.int32, (LANES, CHUNK), 1).astype(F32) + (first_col - centre_col)
     col_gap = col_gap * col_gap
@@ -210,43 +252,57 @@
     return lax.all_to_all(value, axis, split_axis=0, concat_axis=0, tiled=True)
 
 
-def local(spec_re, spec_im, target, weights, cent_row, cent_col):
+def gather_info(info):
+    for bit in (1, 2, 4, 8):
+        info = jnp.concatenate([info, lax.ppermute(info, "src", [(i, i ^ bit) for i in range(16)])], axis=0)
+    return info
+
+
+def compute(spec_re, spec_im, target, weights, cent_row, cent_col):
     rows, band = spec_re.shape
     everyone = ("src", "row")
     row = lax.axis_index("row").astype(jnp.int32).reshape(1)
     src = lax.axis_index("src").astype(jnp.int32).reshape(1)
-    lane = lax.broadcasted_iota(jnp.int32, (16, 8, LANES), 2)
-    info = jnp.where(lane == 1, cent_row.astype(F32)[None, :, None], cent_col.astype(F32)[None, :, None])
-    info = jnp.where(lane == 0, weights[None, :, None], info)
     trig = trig_rows(band)
     table = jax.ShapeDtypeStruct((band, band), BF16)
     parts = jax.ShapeDtypeStruct((16, 32, 8, LANES), BF16)
-    row_block = pl.BlockSpec((CHUNK, band), lambda n: (n, 0))
     col_block = pl.BlockSpec((band, CHUNK), lambda n: (0, n))
-
-    all_info = exchange(info, "src")
-    cosine, sine, column_parts = pl.pallas_call(
+    scalars = (weights, cent_row, cent_col)
+
+    column_parts = pl.pallas_call(
         spectrum_kernel,
-        grid=(STEPS,),
-        in_specs=[SCALARS, WHOLE, WHOLE, WHOLE, WHOLE],
-        out_specs=[row_block, row_block, pl.BlockSpec((16, 8, 8, LANES), lambda n: (0, n, 0, 0))],
-        out_shape=[table, table, parts],
-        scratch_shapes=[pltpu.VMEM((512, 2 * band), BF16), pltpu.VMEM((4 * CHUNK, LANES), F32)],
+        grid=(2,),
+        in_specs=[SCALARS, SCALARS, SCALARS, SCALARS, WHOLE, WHOLE, WHOLE],
+        out_specs=pl.BlockSpec((16, 16, 8, LANES), lambda n: (0, n, 0, 0)),
+        out_shape=parts,
+        scratch_shapes=[
+            pltpu.VMEM((512, 2 * band), BF16),
+            pltpu.VMEM((WIDE, band), BF16),
+            pltpu.VMEM((WIDE, band), BF16),
+            pltpu.VMEM((4 * WIDE, LANES), F32),
+        ],
         name="spectrum",
-    )(row, info, trig, spec_re, spec_im)
-    cos_k, sin_k, cos_y, sin_y = pl.pallas_call(
+    )(row, *scalars, trig, spec_re, spec_im)
+    info, cosine, sine, cos_k, sin_k, cos_y, sin_y = pl.pallas_call(
         tables_kernel,
         grid=(STEPS,),
-        in_specs=[pl.BlockSpec((128, CHUNK), lambda n: (0, n))],
-        out_specs=[col_block] * 4,
-        out_shape=[table] * 4,
-        cost_estimate=pl.CostEstimate(flops=12 * band * band, bytes_accessed=8 * band * band, transcendentals=0),
+        in_specs=[
+            SCALARS,
+            SCALARS,
+            SCALARS,
+            pl.BlockSpec((48, CHUNK), lambda n: (0, n)),
+            pl.BlockSpec(memory_space=pl.ANY),
+        ],
+        out_specs=[WHOLE] + [col_block] * 6,
+        out_shape=[jax.ShapeDtypeStruct((1, 8, LANES), F32)] + [table] * 6,
+        cost_estimate=pl.CostEstimate(flops=18 * band * band, bytes_accessed=12 * band * band, transcendentals=0),
         name="tables",
-    )(trig)
+    )(*scalars, trig, column_parts)
+    all_info = gather_info(info)
     columns = exchange(column_parts.reshape(512, 8, LANES), everyone).reshape(4096, LANES)
     adjoint_parts = pl.pallas_call(
         image_kernel,
-        grid=(2 * STEPS,),
+        grid=(STEPS + 2,),
         in_specs=[
             SCALARS,
             WHOLE,
@@ -254,15 +310,15 @@
             pl.BlockSpec((rows, CHUNK), lambda n: (0, jnp.minimum(n, STEPS - 1))),
             pl.BlockSpec((band, CHUNK), lambda n: (0, jnp.minimum(n, STEPS - 1))),
             pl.BlockSpec((band, CHUNK), lambda n: (0, jnp.minimum(n, STEPS - 1))),
-            pl.BlockSpec((CHUNK, band), lambda n: (jnp.maximum(n - STEPS, 0), 0)),
-            pl.BlockSpec((CHUNK, band), lambda n: (jnp.maximum(n - STEPS, 0), 0)),
-        ],
-        out_specs=pl.BlockSpec((16, 8, 8, LANES), lambda n: (0, jnp.maximum(n - STEPS, 0), 0, 0)),
+            pl.BlockSpec((WIDE, band), lambda n: (jnp.maximum(n - STEPS, 0), 0)),
+            pl.BlockSpec((WIDE, band), lambda n: (jnp.maximum(n - STEPS, 0), 0)),
+        ],
+        out_specs=pl.BlockSpec((16, 16, 8, LANES), lambda n: (0, jnp.maximum(n - STEPS, 0), 0, 0)),
         out_shape=parts,
         scratch_shapes=[
             pltpu.VMEM((512, band), BF16),
             pltpu.VMEM((STEPS, 512, CHUNK), BF16),
-            pltpu.VMEM((4 * CHUNK, LANES), F32),
+            pltpu.VMEM((4 * WIDE, LANES), F32),
         ],
         name="image",
     )(src, all_info, columns, target, cos_k, sin_k, cosine, sine)
@@ -270,7 +326,7 @@
     gradient = pl.pallas_call(
         gradient_kernel,
         grid=(STEPS,),
-        in_specs=[SCALARS, WHOLE, WHOLE, col_block, col_block],
+        in_specs=[SCALARS, SCALARS, WHOLE, WHOLE, col_block, col_block],
         out_specs=WHOLE,
         out_shape=jax.ShapeDtypeStruct((16, 32, LANES), BF16),
         scratch_shapes=[
@@ -279,7 +335,7 @@
             pltpu.VMEM((32, LANES), F32),
         ],
         name="gradient",
-    )(row * rows + 2 * src, all_info.reshape(LANES, LANES), adjoint, cos_y, sin_y)
+    )(row * rows + 2 * src, src, all_info, adjoint, cos_y, sin_y)
     gradient = exchange(gradient, "src").reshape(512, LANES)
     out = jax.ShapeDtypeStruct((rows, band), F32)
     return tuple(
@@ -291,7 +347,7 @@
 
 def solution(mesh):
     return jax.shard_map(
-        local,
+        compute,
         mesh=mesh,
         in_specs=(P("row", None), P("row", None), P("row", None), P("src"), P("src"), P("src")),
         out_specs=(P("row", None), P("row", None)),

time: 152 us -> 155 us (1.020)
  starting transfers between devices: 38.3 us -> 58 us
  waiting for transfers between devices: 60.8 us -> 46.2 us
  other arithmetic: 5.42 us -> 3.54 us
    all_to_all x3 -> x2, waiting for transfers between devices: 60.8 us -> 32.9 us  [exchange(): return lax.all_to_all(value, axis, split_axis=0, concat_axis=0, tiled=True)]
    ppermute x0 -> x4, starting transfers between devices: none -> 14.3 us  [gather_info(): lax.ppermute(info, 'src', [(i, i ^ bit) for i in range(16)])]
    ppermute x0 -> x4, waiting for transfers between devices: none -> 13.4 us  [gather_info(): lax.ppermute(info, 'src', [(i, i ^ bit) for i in range(16)])]
    all_to_all x3 -> x2, starting transfers between devices: 38.3 us -> 43.6 us  [exchange(): return lax.all_to_all(value, axis, split_axis=0, concat_axis=0, tiled=True)]
    concatenate x0 -> x3, other arithmetic: none -> 2.07 us  [gather_info(): jnp.concatenate([info, lax.ppermute(info, 'src', [(i, i ^ bit) for i in r...]
  transfers between devices with their start and end apart: 3 -> 6, of which waited for: 2 -> 5; matrix products, arithmetic and copies ran while one was open for 2% -> 2% of each run, Pallas kernels for 7% -> 4%
where the time goes in v3:
time: 155 us; the launch traced here: 154 us
  starting transfers between devices  58 us (37%)
  waiting for transfers between devices  46.2 us (30%)
  Pallas kernels  29.1 us (19%)
  blocking collectives  13.9 us (9%)
  other arithmetic  3.54 us (2%)
  local copies, waits for them, and re-layouts  2.64 us (2%)
    all_to_all x2, starting transfers between devices, exchange(): return lax.all_to_all(value, axis, split_axis=0, concat_axis=0, tiled=True)  43.6 us
    all_to_all x2, waiting for transfers between devices, exchange(): return lax.all_to_all(value, axis, split_axis=0, concat_axis=0, tiled=True)  32.9 us
    ppermute x4, starting transfers between devices, gather_info(): lax.ppermute(info, 'src', [(i, i ^ bit) for i in range(16)])  14.3 us
    all_to_all x1, blocking collectives, exchange(): return lax.all_to_all(value, axis, split_axis=0, concat_axis=0, tiled=True)  13.9 us
    ppermute x4, waiting for transfers between devices, gather_info(): lax.ppermute(info, 'src', [(i, i ^ bit) for i in range(16)])  13.4 us
    pallas_call x1, Pallas kernels, compute(): pl.pallas_call(image_kernel, grid=(STEPS + 2,), in_specs=[SCALARS, WHOLE,...  10.3 us
    pallas_call x1, Pallas kernels, compute(): pl.pallas_call(gradient_kernel, grid=(STEPS,), in_specs=[SCALARS, SCALARS...  6.37 us
    pallas_call x1, Pallas kernels, compute(): pl.pallas_call(tables_kernel, grid=(STEPS,), in_specs=[SCALARS, SCALARS,...  5.68 us
  transfers between devices with their start and end apart: 6, of which 5 were waited for; matrix products, arithmetic and copies ran while one was open for 2% of the time, Pallas kernels for 4%

profile of v3, /device:TPU:1, one launch (start us, length us, event | category | flops | bytes accessed | tf_op | source)
XLA Modules:
  0.0 154.2 jit_solution(12968806337725488187)
XLA Ops:
  0.6 0.1 iota_multiply_fusion
  0.7 1.4 fusion.3.trig_ref
  2.1 5.1 %spectrum.1._ = bf16[16,32,8,128]{3,2,1,0:T(8,128)(2,1)} custom-call(s32[1]{0:T(128)} %bitcast.row_ref, f32[8]{0:T(128)} %w_ref.3, s32[8]{0:T(128)} %cr_ref.3, s32[8]{0:T(128)} %cc_ref.3, f32[48,1024]{1,0:T(8,128)} %fusion.3.trig_ref, bf16[32,1024]{1,0:T(8,128)(2,1)} %re_ref.1, bf16[32,1024]{1,0:T(8,128)(2,1)} %im_ref.1), custom_call_target="tpu_custom_call" | custom-call | tf_op jit(solution)/shard_map/spectrum/pallas_call | solution.py:272
  7.3 22.2 %all-to-all-start = ((bf16[512,8,128]{2,1,0:T(8,128)(2,1)}), bf16[512,8,128]{2,1,0:T(8,128)(2,1)S(1)}, u32[]{:S(2)}, u32[]{:S(2)}) async-start(bf16[512,8,128]{2,1,0:T(8,128)(2,1)} %bitcast.7), calls=%async_computation | async-start | bytes 2097152 | tf_op jit(solution)/shard_map/all_to_all | solution.py:252
  29.4 5.7 %tables.1 = (f32[1,8,128]{2,1,0:T(8,128)}, bf16[1024,1024]{1,0:T(8,128)(2,1)}, bf16[1024,1024]{1,0:T(8,128)(2,1)}, bf16[1024,1024]{1,0:T(8,128)(2,1)}, bf16[1024...) custom-call(f32[8]{0:T(128)} %w_ref.3, s32[8]{0:T(128)} %cr_ref.3, s32[8]{0:T(128)} %cc_ref.3, ...), custom_call_target="tpu_custom_call" | custom-call | flops 18874368 | bytes 12582912 | tf_op jit(solution)/shard_map/tables/pallas_call | solution.py:286
  35.1 6.2 %collective-permute-start = (f32[1,8,128]{2,1,0:T(8,128)}, f32[1,8,128]{2,1,0:T(8,128)S(1)}, u32[]{:S(2)}, u32[]{:S(2)}) collective-permute-start(f32[1,8,128]{2,1,0:T(8,128)} %get-tuple-element.9), channel_id=1, source_target_pairs={{0,32},{32,0},{64,96},{96,64},{128,160},{160,128},{192,224},{224,1... | collective-permute-start | bytes 12296 | tf_op jit(solution)/shard_map/ppermute | solution.py:257
  41.3 0.7 constant_dynamic-update-slice_fusion.4
  42.0 0.3 collective-permute-done
  42.3 0.7 pad_maximum_fusion.2
  43.0 1.9 %collective-permute-start.1 = (f32[2,8,128]{2,1,0:T(8,128)S(1)}, f32[2,8,128]{2,1,0:T(8,128)S(1)}, u32[]{:S(2)}, u32[]{:S(2)}) collective-permute-start(f32[2,8,128]{2,1,0:T(8,128)S(1)} %pad_maximum_fusion.2), channel_id=1, source_target_pairs={{0,64},{32,96},{64,0},{96,32},{128,192},{160,224},{192,128},{224,1... | collective-permute-start | bytes 24584 | tf_op jit(solution)/shard_map/ppermute | solution.py:257
  44.9 5.0 %collective-permute-done.1 = f32[2,8,128]{2,1,0:T(8,128)S(1)} collective-permute-done((f32[2,8,128]{2,1,0:T(8,128)S(1)}, f32[2,8,128]{2,1,0:T(8,128)S(1)}, u32[]{:S(2)}, u32[]{:S(2)}) %collective-permute-start.1) | collective-permute-done | bytes 8224 | tf_op jit(solution)/shard_map/ppermute | solution.py:257
  49.9 0.7 pad_maximum_fusion.1
  50.6 1.9 %collective-permute-start.2 = (f32[4,8,128]{2,1,0:T(8,128)S(1)}, f32[4,8,128]{2,1,0:T(8,128)S(1)}, u32[]{:S(2)}, u32[]{:S(2)}) collective-permute-start(f32[4,8,128]{2,1,0:T(8,128)S(1)} %pad_maximum_fusion.1), channel_id=1, source_target_pairs={{0,128},{32,160},{64,192},{96,224},{128,0},{160,32},{192,64},{224,... | collective-permute-start | bytes 49160 | tf_op jit(solution)/shard_map/ppermute | solution.py:257
  52.6 3.8 %collective-permute-done.2 = f32[4,8,128]{2,1,0:T(8,128)S(1)} collective-permute-done((f32[4,8,128]{2,1,0:T(8,128)S(1)}, f32[4,8,128]{2,1,0:T(8,128)S(1)}, u32[]{:S(2)}, u32[]{:S(2)}) %collective-permute-start.2) | collective-permute-done | bytes 16416 | tf_op jit(solution)/shard_map/ppermute | solution.py:257
  56.4 0.7 pad_maximum_fusion
  57.1 4.3 %collective-permute-start.3 = (f32[8,8,128]{2,1,0:T(8,128)S(1)}, f32[8,8,128]{2,1,0:T(8,128)S(1)}, u32[]{:S(2)}, u32[]{:S(2)}) collective-permute-start(f32[8,8,128]{2,1,0:T(8,128)S(1)} %pad_maximum_fusion), channel_id=1, source_target_pairs={{0,256},{32,288},{64,320},{96,352},{128,384},{160,416},{192,448},{... | collective-permute-start | bytes 98312 | tf_op jit(solution)/shard_map/ppermute | solution.py:257
  61.4 4.2 %collective-permute-done.3 = f32[8,8,128]{2,1,0:T(8,128)S(1)} collective-permute-done((f32[8,8,128]{2,1,0:T(8,128)S(1)}, f32[8,8,128]{2,1,0:T(8,128)S(1)}, u32[]{:S(2)}, u32[]{:S(2)}) %collective-permute-start.3) | collective-permute-done | bytes 32800 | tf_op jit(solution)/shard_map/ppermute | solution.py:257
  65.6 0.0 copy-start.2
  65.6 0.0 all-to-all-done
  65.6 0.0 copy-start.1
  65.6 0.6 copy-done.2
  66.2 0.4 copy-done.1
  66.6 10.3 %image.1 = bf16[16,32,8,128]{3,2,1,0:T(8,128)(2,1)} custom-call(s32[1]{0:T(128)} %bitcast.1.src_ref, f32[16,8,128]{2,1,0:T(8,128)} %copy-done.2, bf16[4096,128]{1,0:T(8,128)(2,1)} %bitcast.9, f32[32,1024]{1,0:T(8,128)} %target_ref.1, bf16[1024,1024]{1,0:T(8,128)(2,1)} %get-tuple-element.10.cos_k_ref, bf16[1024,1024]{1,0:T(8,128)(2,1)} %get-tuple-element.11.sin_k_ref, ...), custom_call_target="tpu_custom_call" | custom-call | tf_op jit(solution)/shard_map/image/pallas_call | solution.py:303
  76.9 21.5 %all-to-all-start.1 = ((bf16[512,8,128]{2,1,0:T(8,128)(2,1)}), bf16[512,8,128]{2,1,0:T(8,128)(2,1)S(1)}, u32[]{:S(2)}, u32[]{:S(2)}) async-start(bf16[512,8,128]{2,1,0:T(8,128)(2,1)} %bitcast.10), calls=%async_computation.1 | async-start | bytes 2097152 | tf_op jit(solution)/shard_map/all_to_all | solution.py:252
  98.4 32.9 %all-to-all-done.1 = bf16[512,8,128]{2,1,0:T(8,128)(2,1)S(1)} async-done(((bf16[512,8,128]{2,1,0:T(8,128)(2,1)}), bf16[512,8,128]{2,1,0:T(8,128)(2,1)S(1)}, u32[]{:S(2)}, u32[]{:S(2)}) %all-to-all-start.1) | async-done | bytes 1048608 | tf_op jit(solution)/shard_map/all_to_all | solution.py:252
  131.3 0.0 copy-start
  131.3 1.0 copy-done
  132.2 6.4 %gradient.1 = bf16[16,32,128]{2,1,0:T(8,128)(2,1)} custom-call(s32[1]{0:T(128)S(6)} %add.30.place_ref, s32[1]{0:T(128)} %bitcast.1.src_ref, f32[16,8,128]{2,1,0:T(8,128)} %copy-done.2, bf16[4096,128]{1,0:T(8,128)(2,1)} %bitcast.8, bf16[1024,1024]{1,0:T(8,128)(2,1)} %get-tuple-element.14.cos_ref, bf16[1024,1024]{1,0:T(8,128)(2,1)} %get-tuple-element.15.sin_ref), custom_call_target="tpu_custom_call" | custom-call | tf_op jit(solution)/shard_map/gradient/pallas_call | solution.py:326
  138.6 13.9 %all_to_all.15 = bf16[16,32,128]{2,1,0:T(8,128)(2,1)} all-to-all(bf16[16,32,128]{2,1,0:T(8,128)(2,1)} %gradient.1), channel_id=1, replica_groups=mesh['src'=16,'row'=32] {'src'}, dimensions={0} | all-to-all | bytes 262144 | tf_op jit(solution)/shard_map/all_to_all | solution.py:252
  152.5 1.7 %unpack.1 = (f32[32,1024]{1,0:T(8,128)}, f32[32,1024]{1,0:T(8,128)}) custom-call(bf16[512,128]{1,0:T(8,128)(2,1)} %bitcast.11), custom_call_target="tpu_custom_call" | custom-call | tf_op jit(solution)/shard_map/unpack/pallas_call | solution.py:342
  (5 shorter events, 0.0 us)
Async XLA Ops:
  7.3 58.4 %all-to-all-start = ((bf16[512,8,128]{2,1,0:T(8,128)(2,1)}), bf16[512,8,128]{2,1,0:T(8,128)(2,1)S(1)}, u32[]{:S(2)}, u32[]{:S(2)}) async-start(bf16[512,8,128]{2,1,0:T(8,128)(2,1)} %bitcast.7), calls=%async_computation | async-start | bytes 2097152 | tf_op jit(solution)/shard_map/all_to_all | solution.py:252
  35.1 7.2 %collective-permute-start = (f32[1,8,128]{2,1,0:T(8,128)}, f32[1,8,128]{2,1,0:T(8,128)S(1)}, u32[]{:S(2)}, u32[]{:S(2)}) collective-permute-start(f32[1,8,128]{2,1,0:T(8,128)} %get-tuple-element.9), channel_id=1, source_target_pairs={{0,32},{32,0},{64,96},{96,64},{128,160},{160,128},{192,224},{224,1... | collective-permute-start | bytes 12296 | tf_op jit(solution)/shard_map/ppermute | solution.py:257
  43.0 6.9 %collective-permute-start.1 = (f32[2,8,128]{2,1,0:T(8,128)S(1)}, f32[2,8,128]{2,1,0:T(8,128)S(1)}, u32[]{:S(2)}, u32[]{:S(2)}) collective-permute-start(f32[2,8,128]{2,1,0:T(8,128)S(1)} %pad_maximum_fusion.2), channel_id=1, source_target_pairs={{0,64},{32,96},{64,0},{96,32},{128,192},{160,224},{192,128},{224,1... | collective-permute-start | bytes 24584 | tf_op jit(solution)/shard_map/ppermute | solution.py:257
  50.6 5.7 %collective-permute-start.2 = (f32[4,8,128]{2,1,0:T(8,128)S(1)}, f32[4,8,128]{2,1,0:T(8,128)S(1)}, u32[]{:S(2)}, u32[]{:S(2)}) collective-permute-start(f32[4,8,128]{2,1,0:T(8,128)S(1)} %pad_maximum_fusion.1), channel_id=1, source_target_pairs={{0,128},{32,160},{64,192},{96,224},{128,0},{160,32},{192,64},{224,... | collective-permute-start | bytes 49160 | tf_op jit(solution)/shard_map/ppermute | solution.py:257
  57.1 8.6 %collective-permute-start.3 = (f32[8,8,128]{2,1,0:T(8,128)S(1)}, f32[8,8,128]{2,1,0:T(8,128)S(1)}, u32[]{:S(2)}, u32[]{:S(2)}) collective-permute-start(f32[8,8,128]{2,1,0:T(8,128)S(1)} %pad_maximum_fusion), channel_id=1, source_target_pairs={{0,256},{32,288},{64,320},{96,352},{128,384},{160,416},{192,448},{... | collective-permute-start | bytes 98312 | tf_op jit(solution)/shard_map/ppermute | solution.py:257
  65.6 0.6 copy-start.2
  65.6 1.0 copy-start.1
  76.9 54.4 %all-to-all-start.1 = ((bf16[512,8,128]{2,1,0:T(8,128)(2,1)}), bf16[512,8,128]{2,1,0:T(8,128)(2,1)S(1)}, u32[]{:S(2)}, u32[]{:S(2)}) async-start(bf16[512,8,128]{2,1,0:T(8,128)(2,1)} %bitcast.10), calls=%async_computation.1 | async-start | bytes 2097152 | tf_op jit(solution)/shard_map/all_to_all | solution.py:252
  131.3 1.0 copy-start

commit v4 on v3

--- a/solution.py
+++ b/solution.py
@@ -50,7 +50,7 @@
     tile = jnp.zeros(shape, F32)
     for p in range(8):
         centre = jnp.where(lane == 1, cr_ref[p].astype(F32), cc_ref[p].astype(F32))
-        tile = jnp.where(sublane == p, jnp.where(lane == 0, w_ref[p], centre), tile)
+        tile = jnp.where(sublane == p, jnp.where(lane == 0, jnp.sqrt(jnp.full(shape, w_ref[p], F32)), centre), tile)
     return tile
 
 
@@ -93,8 +93,13 @@
             cos_ref[place, :] = cos.astype(BF16)
             sin_ref[place, :] = sin.astype(BF16)
     product = dot_nt(cos_ref[...], lhs_ref[:, :band]) + dot_nt(sin_ref[...], lhs_ref[:, band:])
+    point = lax.broadcasted_iota(jnp.int32, (8, LANES), 1) % 8
+    root = jnp.zeros((8, LANES), F32)
+    for p in range(8):
+        root = jnp.where(point == p, w_ref[p], root)
+    root = jnp.sqrt(root)[0:1, :]
     for t in range(4):
-        flat_ref[pl.ds(t, WIDE, stride=4), :] = product[:, t * LANES : (t + 1) * LANES]
+        flat_ref[pl.ds(t, WIDE, stride=4), :] = product[:, t * LANES : (t + 1) * LANES] * root
     low_row = lax.broadcasted_iota(jnp.int32, (8, LANES), 0) < 4
     low_lane = lax.broadcasted_iota(jnp.int32, (8, LANES), 1) < 64
     stay = low_row == low_lane
@@ -141,15 +146,25 @@
 
 
 def image_kernel(
-    src_ref, info_ref, in_ref, target_ref, cos_k_ref, sin_k_ref, cos_ref, sin_ref, out_ref, lhs_ref, grad_ref, flat_ref
+    src_ref,
+    info_ref,
+    in_ref,
+    target_ref,
+    cos_k_ref,
+    sin_k_ref,
+    cos_ref,
+    sin_ref,
+    out_ref,
+    info_out_ref,
+    lhs_ref,
+    grad_ref,
+    flat_ref,
 ):
     step = pl.program_id(0)
 
-    def weight(s):
-        return info_ref[jnp.bitwise_xor(src_ref[0], s)][:, 0:1]
-
     @pl.when(step == 0)
     def _():
+        info_out_ref[...] = info_ref[...]
         for s in range(16):
             turned = in_ref[256 * s : 256 * s + 256, :].T
             for y in range(2):
@@ -173,14 +188,14 @@
             power = jnp.zeros((8, CHUNK), F32)
             for s in range(16):
                 re, im = field(s, y)
-                power += weight(s) * (re * re + im * im)
+                power += re * re + im * im
             intensity = jnp.sum(power, axis=0, keepdims=True) * (1.0 / 128.0)
             mismatch = intensity - target_ref[pl.ds(2 * src_ref[0] + y, 1), :]
+            factor = 2.0 * mismatch
             for s in range(0, 16, 2):
                 grads_re, grads_im = [], []
                 for one in (s, s + 1):
                     re, im = field(one, y)
-                    factor = (2.0 * weight(one)) * mismatch
                     grads_re.append(factor * re)
                     grads_im.append(factor * im)
                 at = 256 * y + 8 * s
@@ -221,17 +236,18 @@
     by_cos = dot_nn(lhs_ref[...], cos_ref[...])
     by_sin = dot_nn(lhs_ref[...], sin_ref[...])
     info = jnp.concatenate([info_ref[jnp.bitwise_xor(src_ref[0], s)] for s in range(16)], axis=0)
-    centre_row, centre_col = info[:, 1:2], info[:, 2:3]
+    root, centre_row, centre_col = info[:, 0:1], info[:, 1:2], info[:, 2:3]
     first_col = (step * CHUNK).astype(F32)
     col_gap = lax.broadcasted_iota(jnp.int32, (LANES, CHUNK), 1).astype(F32) + (first_col - centre_col)
     col_gap = col_gap * col_gap
     for k in range(2):
         row_gap = (place_ref[0] + k).astype(F32) - centre_row
         keep = row_gap * row_gap + col_gap <= float(RAD * RAD)
+        factor = jnp.where(keep, root, 0.0)
         re, im = slice(128 * k, 128 * k + 128), slice(256 + 128 * k, 256 + 128 * k + 128)
         terms = (by_cos[re] + by_sin[im], by_cos[im] - by_sin[re])
         for c in range(2):
-            total = jnp.sum(jnp.where(keep, terms[c], 0.0), axis=0, keepdims=True)
+            total = jnp.sum(factor * terms[c], axis=0, keepdims=True)
             for side in range(2):
                 sums_ref[pl.ds(16 * k + 8 * c + 2 * step + side, 1), :] = total[:, side * LANES : (side + 1) * LANES]
 
@@ -252,8 +268,8 @@
     return lax.all_to_all(value, axis, split_axis=0, concat_axis=0, tiled=True)
 
 
-def gather_info(info):
-    for bit in (1, 2, 4, 8):
+def gather_info(info, bits):
+    for bit in bits:
         info = jnp.concatenate([info, lax.ppermute(info, "src", [(i, i ^ bit) for i in range(16)])], axis=0)
     return info
 
@@ -298,9 +314,9 @@
         cost_estimate=pl.CostEstimate(flops=18 * band * band, bytes_accessed=12 * band * band, transcendentals=0),
         name="tables",
     )(*scalars, trig, column_parts)
-    all_info = gather_info(info)
+    some_info = gather_info(info, (1, 2))
     columns = exchange(column_parts.reshape(512, 8, LANES), everyone).reshape(4096, LANES)
-    adjoint_parts = pl.pallas_call(
+    adjoint_parts, some_info = pl.pallas_call(
         image_kernel,
         grid=(STEPS + 2,),
         in_specs=[
@@ -313,16 +329,17 @@
             pl.BlockSpec((WIDE, band), lambda n: (jnp.maximum(n - STEPS, 0), 0)),
             pl.BlockSpec((WIDE, band), lambda n: (jnp.maximum(n - STEPS, 0), 0)),
         ],
-        out_specs=pl.BlockSpec((16, 16, 8, LANES), lambda n: (0, jnp.maximum(n - STEPS, 0), 0, 0)),
-        out_shape=parts,
+        out_specs=[pl.BlockSpec((16, 16, 8, LANES), lambda n: (0, jnp.maximum(n - STEPS, 0), 0, 0)), WHOLE],
+        out_shape=[parts, jax.ShapeDtypeStruct((4, 8, LANES), F32)],
         scratch_shapes=[
             pltpu.VMEM((512, band), BF16),
             pltpu.VMEM((STEPS, 512, CHUNK), BF16),
             pltpu.VMEM((4 * WIDE, LANES), F32),
         ],
         name="image",
-    )(src, all_info, columns, target, cos_k, sin_k, cosine, sine)
+    )(src, some_info, columns, target, cos_k, sin_k, cosine, sine)
     adjoint = exchange(adjoint_parts.reshape(512, 8, LANES), everyone).reshape(4096, LANES)
+    all_info = gather_info(some_info, (4, 8))
     gradient = pl.pallas_call(
         gradient_kernel,
         grid=(STEPS,),

time: 155 us -> 141 us (0.910); the launches traced: 154 us -> 138 us
  waiting for transfers between devices: 46.2 us -> 33.1 us
  starting transfers between devices: 58 us -> 55.7 us
    all_to_all x2, waiting for transfers between devices: 32.9 us -> 13.8 us  [exchange(): return lax.all_to_all(value, axis, split_axis=0, concat_axis=0, tiled=True)]
    all_to_all x2, starting transfers between devices: 43.6 us -> 31.2 us  [exchange(): return lax.all_to_all(value, axis, split_axis=0, concat_axis=0, tiled=True)]
    ppermute x4, starting transfers between devices: 14.3 us -> 24.4 us  [gather_info(): lax.ppermute(info, 'src', [(i, i ^ bit) for i in range(16)])]
    ppermute x4, waiting for transfers between devices: 13.4 us -> 19.3 us  [gather_info(): lax.ppermute(info, 'src', [(i, i ^ bit) for i in range(16)])]
  transfers between devices with their start and end apart: 6 -> 6, of which waited for: 5 -> 6; matrix products, arithmetic and copies ran while one was open for 2% -> 2% of each run, Pallas kernels for 4% -> 4%
where the time goes in v4:
time: 141 us; the launch traced here: 138 us
  starting transfers between devices  55.7 us (40%)
  waiting for transfers between devices  33.1 us (23%)
  Pallas kernels  29 us (21%)
  blocking collectives  13.9 us (10%)
  other arithmetic  4.09 us (3%)
  local copies, waits for them, and re-layouts  1.95 us (1%)
    all_to_all x2, starting transfers between devices, exchange(): return lax.all_to_all(value, axis, split_axis=0, concat_axis=0, tiled=True)  31.2 us
    ppermute x4, starting transfers between devices, gather_info(): lax.ppermute(info, 'src', [(i, i ^ bit) for i in range(16)])  24.4 us
    ppermute x4, waiting for transfers between devices, gather_info(): lax.ppermute(info, 'src', [(i, i ^ bit) for i in range(16)])  19.3 us
    all_to_all x1, blocking collectives, exchange(): return lax.all_to_all(value, axis, split_axis=0, concat_axis=0, tiled=True)  13.9 us
    all_to_all x2, waiting for transfers between devices, exchange(): return lax.all_to_all(value, axis, split_axis=0, concat_axis=0, tiled=True)  13.8 us
    pallas_call x1, Pallas kernels, compute(): pl.pallas_call(image_kernel, grid=(STEPS + 2,), in_specs=[SCALARS, WHOLE,...  10.2 us
    pallas_call x1, Pallas kernels, compute(): pl.pallas_call(gradient_kernel, grid=(STEPS,), in_specs=[SCALARS, SCALARS...  6.37 us
    pallas_call x1, Pallas kernels, compute(): pl.pallas_call(tables_kernel, grid=(STEPS,), in_specs=[SCALARS, SCALARS,...  5.69 us
  transfers between devices with their start and end apart: 6, of which 6 were waited for; matrix products, arithmetic and copies ran while one was open for 2% of the time, Pallas kernels for 4%

profile of v4, /device:TPU:1, one launch (start us, length us, event | category | flops | bytes accessed | tf_op | source)
XLA Modules:
  0.0 138.5 jit_solution(11271135908345268714)
XLA Ops:
  0.6 0.1 iota_multiply_fusion
  0.7 1.4 fusion.3.trig_ref
  2.1 5.1 %spectrum.1._ = bf16[16,32,8,128]{3,2,1,0:T(8,128)(2,1)} custom-call(s32[1]{0:T(128)} %bitcast.row_ref, f32[8]{0:T(128)} %w_ref.3, s32[8]{0:T(128)} %cr_ref.3, s32[8]{0:T(128)} %cc_ref.3, f32[48,1024]{1,0:T(8,128)} %fusion.3.trig_ref, bf16[32,1024]{1,0:T(8,128)(2,1)} %re_ref.1, bf16[32,1024]{1,0:T(8,128)(2,1)} %im_ref.1), custom_call_target="tpu_custom_call" | custom-call | tf_op jit(solution)/shard_map/spectrum/pallas_call | solution.py:288
  7.2 22.1 %all-to-all-start = ((bf16[512,8,128]{2,1,0:T(8,128)(2,1)}), bf16[512,8,128]{2,1,0:T(8,128)(2,1)S(1)}, u32[]{:S(2)}, u32[]{:S(2)}) async-start(bf16[512,8,128]{2,1,0:T(8,128)(2,1)} %bitcast.7), calls=%async_computation | async-start | bytes 2097152 | tf_op jit(solution)/shard_map/all_to_all | solution.py:268
  29.4 5.7 %tables.1 = (f32[1,8,128]{2,1,0:T(8,128)}, bf16[1024,1024]{1,0:T(8,128)(2,1)}, bf16[1024,1024]{1,0:T(8,128)(2,1)}, bf16[1024,1024]{1,0:T(8,128)(2,1)}, bf16[1024...) custom-call(f32[8]{0:T(128)} %w_ref.3, s32[8]{0:T(128)} %cr_ref.3, s32[8]{0:T(128)} %cc_ref.3, ...), custom_call_target="tpu_custom_call" | custom-call | flops 18874368 | bytes 12582912 | tf_op jit(solution)/shard_map/tables/pallas_call | solution.py:302
  35.1 6.2 %collective-permute-start = (f32[1,8,128]{2,1,0:T(8,128)}, f32[1,8,128]{2,1,0:T(8,128)S(1)}, u32[]{:S(2)}, u32[]{:S(2)}) collective-permute-start(f32[1,8,128]{2,1,0:T(8,128)} %get-tuple-element.11), channel_id=1, source_target_pairs={{0,32},{32,0},{64,96},{96,64},{128,160},{160,128},{192,224},{224,1... | collective-permute-start | bytes 12296 | tf_op jit(solution)/shard_map/ppermute | solution.py:273
  41.3 1.0 collective-permute-done
  42.3 0.7 pad_maximum_fusion.3
  43.0 1.9 %collective-permute-start.1 = (f32[2,8,128]{2,1,0:T(8,128)S(1)}, f32[2,8,128]{2,1,0:T(8,128)S(1)}, u32[]{:S(2)}, u32[]{:S(2)}) collective-permute-start(f32[2,8,128]{2,1,0:T(8,128)S(1)} %pad_maximum_fusion.3), channel_id=1, source_target_pairs={{0,64},{32,96},{64,0},{96,32},{128,192},{160,224},{192,128},{224,1... | collective-permute-start | bytes 24584 | tf_op jit(solution)/shard_map/ppermute | solution.py:273
  44.9 5.0 %collective-permute-done.1 = f32[2,8,128]{2,1,0:T(8,128)S(1)} collective-permute-done((f32[2,8,128]{2,1,0:T(8,128)S(1)}, f32[2,8,128]{2,1,0:T(8,128)S(1)}, u32[]{:S(2)}, u32[]{:S(2)}) %collective-permute-start.1) | collective-permute-done | bytes 8224 | tf_op jit(solution)/shard_map/ppermute | solution.py:273
  49.9 1.3 pad_maximum_fusion.2.info_ref
  51.2 11.0 %all-to-all-done = bf16[512,8,128]{2,1,0:T(8,128)(2,1)S(1)} async-done(((bf16[512,8,128]{2,1,0:T(8,128)(2,1)}), bf16[512,8,128]{2,1,0:T(8,128)(2,1)S(1)}, u32[]{:S(2)}, u32[]{:S(2)}) %all-to-all-start) | async-done | bytes 1048608 | tf_op jit(solution)/shard_map/all_to_all | solution.py:268
  62.2 0.0 copy-start
  62.2 1.0 copy-done
  63.2 10.2 %image.1 = (bf16[16,32,8,128]{3,2,1,0:T(8,128)(2,1)}, f32[4,8,128]{2,1,0:T(8,128)}) custom-call(s32[1]{0:T(128)} %bitcast.1.src_ref, f32[4,8,128]{2,1,0:T(8,128)} %pad_maximum_fusion.2.info_ref, bf16[4096,128]{1,0:T(8,128)(2,1)} %bitcast.8, f32[32,1024]{1,0:T(8,128)} %target_ref.1, bf16[1024,1024]{1,0:T(8,128)(2,1)} %get-tuple-element.12.cos_k_ref, ...), custom_call_target="tpu_custom_call" | custom-call | tf_op jit(solution)/shard_map/image/pallas_call | solution.py:319
  73.4 0.0 copy-start.2
  73.4 9.1 %all-to-all-start.1 = ((bf16[512,8,128]{2,1,0:T(8,128)(2,1)}), bf16[512,8,128]{2,1,0:T(8,128)(2,1)S(1)}, u32[]{:S(2)}, u32[]{:S(2)}) async-start(bf16[512,8,128]{2,1,0:T(8,128)(2,1)} %bitcast.10), calls=%async_computation.1 | async-start | bytes 2097152 | tf_op jit(solution)/shard_map/all_to_all | solution.py:268
  82.5 0.0 copy-done.2
  82.5 5.2 %collective-permute-start.2 = (f32[4,8,128]{2,1,0:T(8,128)S(1)}, f32[4,8,128]{2,1,0:T(8,128)S(1)}, u32[]{:S(2)}, u32[]{:S(2)}) collective-permute-start(f32[4,8,128]{2,1,0:T(8,128)S(1)} %copy-done.2), channel_id=1, source_target_pairs={{0,128},{32,160},{64,192},{96,224},{128,0},{160,32},{192,64},{224,... | collective-permute-start | bytes 49160 | tf_op jit(solution)/shard_map/ppermute | solution.py:273
  87.8 7.6 %collective-permute-done.2 = f32[4,8,128]{2,1,0:T(8,128)S(1)} collective-permute-done((f32[4,8,128]{2,1,0:T(8,128)S(1)}, f32[4,8,128]{2,1,0:T(8,128)S(1)}, u32[]{:S(2)}, u32[]{:S(2)}) %collective-permute-start.2) | collective-permute-done | bytes 16416 | tf_op jit(solution)/shard_map/ppermute | solution.py:273
  95.4 11.1 %collective-permute-start.3 = (f32[8,8,128]{2,1,0:T(8,128)S(1)}, f32[8,8,128]{2,1,0:T(8,128)S(1)}, u32[]{:S(2)}, u32[]{:S(2)}) collective-permute-start(f32[8,8,128]{2,1,0:T(8,128)S(1)} %pad_maximum_fusion.1), channel_id=1, source_target_pairs={{0,256},{32,288},{64,320},{96,352},{128,384},{160,416},{192,448},{... | collective-permute-start | bytes 98312 | tf_op jit(solution)/shard_map/ppermute | solution.py:273
  106.5 5.7 %collective-permute-done.3 = f32[8,8,128]{2,1,0:T(8,128)S(1)} collective-permute-done((f32[8,8,128]{2,1,0:T(8,128)S(1)}, f32[8,8,128]{2,1,0:T(8,128)S(1)}, u32[]{:S(2)}, u32[]{:S(2)}) %collective-permute-start.3) | collective-permute-done | bytes 32800 | tf_op jit(solution)/shard_map/ppermute | solution.py:273
  112.2 0.6 pad_maximum_fusion.info_ref
  112.8 2.7 %all-to-all-done.1 = bf16[512,8,128]{2,1,0:T(8,128)(2,1)S(1)} async-done(((bf16[512,8,128]{2,1,0:T(8,128)(2,1)}), bf16[512,8,128]{2,1,0:T(8,128)(2,1)S(1)}, u32[]{:S(2)}, u32[]{:S(2)}) %all-to-all-start.1) | async-done | bytes 1048608 | tf_op jit(solution)/shard_map/all_to_all | solution.py:268
  115.5 0.0 copy-start.1
  115.5 1.0 copy-done.1
  116.5 6.4 %gradient.1 = bf16[16,32,128]{2,1,0:T(8,128)(2,1)} custom-call(s32[1]{0:T(128)S(6)} %add.30.place_ref, s32[1]{0:T(128)} %bitcast.1.src_ref, f32[16,8,128]{2,1,0:T(8,128)} %pad_maximum_fusion.info_ref, bf16[4096,128]{1,0:T(8,128)(2,1)} %bitcast.9, bf16[1024,1024]{1,0:T(8,128)(2,1)} %get-tuple-element.18.cos_ref, bf16[1024,1024]{1,0:T(8,128)(2,1)} %get-tuple-element.19.sin_ref), custom_call_target="tpu_custom_call" | custom-call | tf_op jit(solution)/shard_map/gradient/pallas_call | solution.py:343
  122.9 13.9 %all_to_all.15 = bf16[16,32,128]{2,1,0:T(8,128)(2,1)} all-to-all(bf16[16,32,128]{2,1,0:T(8,128)(2,1)} %gradient.1), channel_id=1, replica_groups=mesh['src'=16,'row'=32] {'src'}, dimensions={0} | all-to-all | bytes 262144 | tf_op jit(solution)/shard_map/all_to_all | solution.py:268
  136.8 1.7 %unpack.1 = (f32[32,1024]{1,0:T(8,128)}, f32[32,1024]{1,0:T(8,128)}) custom-call(bf16[512,128]{1,0:T(8,128)(2,1)} %bitcast.11), custom_call_target="tpu_custom_call" | custom-call | tf_op jit(solution)/shard_map/unpack/pallas_call | solution.py:359
  (2 shorter events, 0.0 us)
Async XLA Ops:
  7.2 55.0 %all-to-all-start = ((bf16[512,8,128]{2,1,0:T(8,128)(2,1)}), bf16[512,8,128]{2,1,0:T(8,128)(2,1)S(1)}, u32[]{:S(2)}, u32[]{:S(2)}) async-start(bf16[512,8,128]{2,1,0:T(8,128)(2,1)} %bitcast.7), calls=%async_computation | async-start | bytes 2097152 | tf_op jit(solution)/shard_map/all_to_all | solution.py:268
  35.1 7.2 %collective-permute-start = (f32[1,8,128]{2,1,0:T(8,128)}, f32[1,8,128]{2,1,0:T(8,128)S(1)}, u32[]{:S(2)}, u32[]{:S(2)}) collective-permute-start(f32[1,8,128]{2,1,0:T(8,128)} %get-tuple-element.11), channel_id=1, source_target_pairs={{0,32},{32,0},{64,96},{96,64},{128,160},{160,128},{192,224},{224,1... | collective-permute-start | bytes 12296 | tf_op jit(solution)/shard_map/ppermute | solution.py:273
  43.0 6.9 %collective-permute-start.1 = (f32[2,8,128]{2,1,0:T(8,128)S(1)}, f32[2,8,128]{2,1,0:T(8,128)S(1)}, u32[]{:S(2)}, u32[]{:S(2)}) collective-permute-start(f32[2,8,128]{2,1,0:T(8,128)S(1)} %pad_maximum_fusion.3), channel_id=1, source_target_pairs={{0,64},{32,96},{64,0},{96,32},{128,192},{160,224},{192,128},{224,1... | collective-permute-start | bytes 24584 | tf_op jit(solution)/shard_map/ppermute | solution.py:273
  62.2 1.0 copy-start
  73.4 9.1 %copy-start.2 = (f32[4,8,128]{2,1,0:T(8,128)S(1)}, f32[4,8,128]{2,1,0:T(8,128)}, u32[]{:S(2)}) copy-start(f32[4,8,128]{2,1,0:T(8,128)} %get-tuple-element.16) | copy-start | bytes 49156
  73.4 42.1 %all-to-all-start.1 = ((bf16[512,8,128]{2,1,0:T(8,128)(2,1)}), bf16[512,8,128]{2,1,0:T(8,128)(2,1)S(1)}, u32[]{:S(2)}, u32[]{:S(2)}) async-start(bf16[512,8,128]{2,1,0:T(8,128)(2,1)} %bitcast.10), calls=%async_computation.1 | async-start | bytes 2097152 | tf_op jit(solution)/shard_map/all_to_all | solution.py:268
  82.5 12.9 %collective-permute-start.2 = (f32[4,8,128]{2,1,0:T(8,128)S(1)}, f32[4,8,128]{2,1,0:T(8,128)S(1)}, u32[]{:S(2)}, u32[]{:S(2)}) collective-permute-start(f32[4,8,128]{2,1,0:T(8,128)S(1)} %copy-done.2), channel_id=1, source_target_pairs={{0,128},{32,160},{64,192},{96,224},{128,0},{160,32},{192,64},{224,... | collective-permute-start | bytes 49160 | tf_op jit(solution)/shard_map/ppermute | solution.py:273
  95.4 16.8 %collective-permute-start.3 = (f32[8,8,128]{2,1,0:T(8,128)S(1)}, f32[8,8,128]{2,1,0:T(8,128)S(1)}, u32[]{:S(2)}, u32[]{:S(2)}) collective-permute-start(f32[8,8,128]{2,1,0:T(8,128)S(1)} %pad_maximum_fusion.1), channel_id=1, source_target_pairs={{0,256},{32,288},{64,320},{96,352},{128,384},{160,416},{192,448},{... | collective-permute-start | bytes 98312 | tf_op jit(solution)/shard_map/ppermute | solution.py:273
  115.5 1.0 copy-start.1

commit v5 on v4

--- a/solution.py
+++ b/solution.py
@@ -62,7 +62,7 @@
     return jnp.dot(left, right, preferred_element_type=F32)
 
 
-def spectrum_kernel(row_ref, w_ref, cr_ref, cc_ref, trig_ref, re_ref, im_ref, out_ref, lhs_ref, cos_ref, sin_ref, flat_ref):
+def spectrum_kernel(row_ref, w_ref, cr_ref, cc_ref, trig_ref, re_ref, im_ref, out_ref, lhs_ref, table_ref, flat_ref):
     step = pl.program_id(0)
     rows, band = re_ref.shape
 
@@ -90,9 +90,9 @@
         for d in range(4):
             cos, sin = rotate(rotate(coarse, pick(trig_ref, 20 + d)), base)
             place = slice(128 * a + 32 * d, 128 * a + 32 * d + 32)
-            cos_ref[place, :] = cos.astype(BF16)
-            sin_ref[place, :] = sin.astype(BF16)
-    product = dot_nt(cos_ref[...], lhs_ref[:, :band]) + dot_nt(sin_ref[...], lhs_ref[:, band:])
+            table_ref[place, :band] = cos.astype(BF16)
+            table_ref[place, band:] = sin.astype(BF16)
+    product = dot_nt(table_ref[...], lhs_ref[...])
     point = lax.broadcasted_iota(jnp.int32, (8, LANES), 1) % 8
     root = jnp.zeros((8, LANES), F32)
     for p in range(8):
@@ -178,6 +178,8 @@
         by_cos = dot_nn(lhs_ref[...], cos_k_ref[...])
         by_sin = dot_nn(lhs_ref[...], sin_k_ref[...])
 
+        cols = pl.ds(pl.multiple_of(step * CHUNK, CHUNK), CHUNK)
+
         def field(s, y):
             at = 32 * s + 16 * y
             re = by_cos[at : at + 8] - by_sin[at + 8 : at + 16]
@@ -199,17 +201,13 @@
                     grads_re.append(factor * re)
                     grads_im.append(factor * im)
                 at = 256 * y + 8 * s
-                grad_ref[step, at : at + 16, :] = jnp.concatenate(grads_re, axis=0).astype(BF16)
-                grad_ref[step, at + 128 : at + 144, :] = jnp.concatenate(grads_im, axis=0).astype(BF16)
+                grad_ref[at : at + 16, cols] = jnp.concatenate(grads_re, axis=0).astype(BF16)
+                grad_ref[at + 128 : at + 144, cols] = jnp.concatenate(grads_im, axis=0).astype(BF16)
 
     @pl.when(step >= STEPS)
     def _():
-        by_cos = jnp.zeros((WIDE, 512), F32)
-        by_sin = jnp.zeros((WIDE, 512), F32)
-        for n in range(STEPS):
-            cols = slice(n * CHUNK, (n + 1) * CHUNK)
-            by_cos += dot_nt(cos_ref[:, cols], grad_ref[n])
-            by_sin += dot_nt(sin_ref[:, cols], grad_ref[n])
+        by_cos = dot_nt(cos_ref[...], grad_ref[...])
+        by_sin = dot_nt(sin_ref[...], grad_ref[...])
         for y in range(2):
             re, im = slice(256 * y, 256 * y + 128), slice(256 * y + 128, 256 * y + 256)
             flat_ref[pl.ds(2 * y, WIDE, stride=4), :] = by_cos[:, re] + by_sin[:, im]
@@ -231,11 +229,12 @@
             for y in range(2):
                 for c in range(2):
                     part = flat_ref[pl.ds(4 * k + 2 * y + c, 512, stride=8), :]
-                    lhs_ref[128 * (2 * c + k) : 128 * (2 * c + k) + 128, 512 * y : 512 * y + 512] = part.T.astype(BF16)
+                    lhs_ref[128 * (2 * c + k) : 128 * (2 * c + k) + 128, 512 * y : 512 * y + 512] = part.astype(BF16).T
 
     by_cos = dot_nn(lhs_ref[...], cos_ref[...])
     by_sin = dot_nn(lhs_ref[...], sin_ref[...])
-    info = jnp.concatenate([info_ref[jnp.bitwise_xor(src_ref[0], s)] for s in range(16)], axis=0)
+    gaps = [jnp.bitwise_xor(src_ref[0], s) for s in range(16)]
+    info = jnp.concatenate([info_ref[gap // 2 + 8 * (gap % 2)] for gap in gaps], axis=0)
     root, centre_row, centre_col = info[:, 0:1], info[:, 1:2], info[:, 2:3]
     first_col = (step * CHUNK).astype(F32)
     col_gap = lax.broadcasted_iota(jnp.int32, (LANES, CHUNK), 1).astype(F32) + (first_col - centre_col)
@@ -293,8 +292,7 @@
         out_shape=parts,
         scratch_shapes=[
             pltpu.VMEM((512, 2 * band), BF16),
-            pltpu.VMEM((WIDE, band), BF16),
-            pltpu.VMEM((WIDE, band), BF16),
+            pltpu.VMEM((WIDE, 2 * band), BF16),
             pltpu.VMEM((4 * WIDE, LANES), F32),
         ],
         name="spectrum",
@@ -314,7 +312,7 @@
         cost_estimate=pl.CostEstimate(flops=18 * band * band, bytes_accessed=12 * band * band, transcendentals=0),
         name="tables",
     )(*scalars, trig, column_parts)
-    some_info = gather_info(info, (1, 2))
+    some_info = gather_info(info, (2, 4))
     columns = exchange(column_parts.reshape(512, 8, LANES), everyone).reshape(4096, LANES)
     adjoint_parts, some_info = pl.pallas_call(
         image_kernel,
@@ -333,13 +331,13 @@
         out_shape=[parts, jax.ShapeDtypeStruct((4, 8, LANES), F32)],
         scratch_shapes=[
             pltpu.VMEM((512, band), BF16),
-            pltpu.VMEM((STEPS, 512, CHUNK), BF16),
+            pltpu.VMEM((512, band), BF16),
             pltpu.VMEM((4 * WIDE, LANES), F32),
         ],
         name="image",
     )(src, some_info, columns, target, cos_k, sin_k, cosine, sine)
     adjoint = exchange(adjoint_parts.reshape(512, 8, LANES), everyone).reshape(4096, LANES)
-    all_info = gather_info(some_info, (4, 8))
+    all_info = gather_info(some_info, (8, 1))
     gradient = pl.pallas_call(
         gradient_kernel,
         grid=(STEPS,),

time: 141 us -> 145 us (1.028); the launches traced: 138 us -> 145 us
  starting transfers between devices: 55.7 us -> 59.3 us
  waiting for transfers between devices: 33.1 us -> 35.5 us
    all_to_all x2, starting transfers between devices: 31.2 us -> 37.4 us  [exchange(): return lax.all_to_all(value, axis, split_axis=0, concat_axis=0, tiled=True)]
    all_to_all x2, waiting for transfers between devices: 13.8 us -> 17 us  [exchange(): return lax.all_to_all(value, axis, split_axis=0, concat_axis=0, tiled=True)]
    ppermute x4, starting transfers between devices: 24.4 us -> 21.9 us  [gather_info(): lax.ppermute(info, 'src', [(i, i ^ bit) for i in range(16)])]
where the time goes in v5:
time: 145 us
  starting transfers between devices  59.3 us (41%)
  waiting for transfers between devices  35.5 us (24%)
  Pallas kernels  29 us (20%)
  blocking collectives  13.9 us (10%)
  other arithmetic  4.09 us (3%)
  local copies, waits for them, and re-layouts  1.95 us (1%)
    all_to_all x2, starting transfers between devices, exchange(): return lax.all_to_all(value, axis, split_axis=0, concat_axis=0, tiled=True)  37.4 us
    ppermute x4, starting transfers between devices, gather_info(): lax.ppermute(info, 'src', [(i, i ^ bit) for i in range(16)])  21.9 us
    ppermute x4, waiting for transfers between devices, gather_info(): lax.ppermute(info, 'src', [(i, i ^ bit) for i in range(16)])  18.5 us
    all_to_all x2, waiting for transfers between devices, exchange(): return lax.all_to_all(value, axis, split_axis=0, concat_axis=0, tiled=True)  17 us
    all_to_all x1, blocking collectives, exchange(): return lax.all_to_all(value, axis, split_axis=0, concat_axis=0, tiled=True)  13.9 us
    pallas_call x1, Pallas kernels, compute(): pl.pallas_call(image_kernel, grid=(STEPS + 2,), in_specs=[SCALARS, WHOLE,...  10.2 us
    pallas_call x1, Pallas kernels, compute(): pl.pallas_call(gradient_kernel, grid=(STEPS,), in_specs=[SCALARS, SCALARS...  6.35 us
    pallas_call x1, Pallas kernels, compute(): pl.pallas_call(tables_kernel, grid=(STEPS,), in_specs=[SCALARS, SCALARS,...  5.69 us
  transfers between devices with their start and end apart: 6, of which 6 were waited for; matrix products, arithmetic and copies ran while one was open for 2% of the time, Pallas kernels for 4%

profile of v5, /device:TPU:1, one launch (start us, length us, event | category | flops | bytes accessed | tf_op | source)
XLA Modules:
  0.0 144.6 jit_solution(3140880530952443797)
XLA Ops:
  0.6 0.1 iota_multiply_fusion
  0.7 1.4 fusion.3.trig_ref
  2.1 5.1 %spectrum.1._ = bf16[16,32,8,128]{3,2,1,0:T(8,128)(2,1)} custom-call(s32[1]{0:T(128)} %bitcast.row_ref, f32[8]{0:T(128)} %w_ref.3, s32[8]{0:T(128)} %cr_ref.3, s32[8]{0:T(128)} %cc_ref.3, f32[48,1024]{1,0:T(8,128)} %fusion.3.trig_ref, bf16[32,1024]{1,0:T(8,128)(2,1)} %re_ref.1, bf16[32,1024]{1,0:T(8,128)(2,1)} %im_ref.1), custom_call_target="tpu_custom_call" | custom-call | tf_op jit(solution)/shard_map/spectrum/pallas_call | solution.py:287
  7.2 22.1 %all-to-all-start = ((bf16[512,8,128]{2,1,0:T(8,128)(2,1)}), bf16[512,8,128]{2,1,0:T(8,128)(2,1)S(1)}, u32[]{:S(2)}, u32[]{:S(2)}) async-start(bf16[512,8,128]{2,1,0:T(8,128)(2,1)} %bitcast.7), calls=%async_computation | async-start | bytes 2097152 | tf_op jit(solution)/shard_map/all_to_all | solution.py:267
  29.4 5.7 %tables.1 = (f32[1,8,128]{2,1,0:T(8,128)}, bf16[1024,1024]{1,0:T(8,128)(2,1)}, bf16[1024,1024]{1,0:T(8,128)(2,1)}, bf16[1024,1024]{1,0:T(8,128)(2,1)}, bf16[1024...) custom-call(f32[8]{0:T(128)} %w_ref.3, s32[8]{0:T(128)} %cr_ref.3, s32[8]{0:T(128)} %cc_ref.3, ...), custom_call_target="tpu_custom_call" | custom-call | flops 18874368 | bytes 12582912 | tf_op jit(solution)/shard_map/tables/pallas_call | solution.py:300
  35.1 3.6 %collective-permute-start = (f32[1,8,128]{2,1,0:T(8,128)}, f32[1,8,128]{2,1,0:T(8,128)S(1)}, u32[]{:S(2)}, u32[]{:S(2)}) collective-permute-start(f32[1,8,128]{2,1,0:T(8,128)} %get-tuple-element.11), channel_id=1, source_target_pairs={{0,64},{32,96},{64,0},{96,32},{128,192},{160,224},{192,128},{224,1... | collective-permute-start | bytes 12296 | tf_op jit(solution)/shard_map/ppermute | solution.py:272
  38.7 3.3 %collective-permute-done = f32[1,8,128]{2,1,0:T(8,128)S(1)} collective-permute-done((f32[1,8,128]{2,1,0:T(8,128)}, f32[1,8,128]{2,1,0:T(8,128)S(1)}, u32[]{:S(2)}, u32[]{:S(2)}) %collective-permute-start) | collective-permute-done | bytes 4128 | tf_op jit(solution)/shard_map/ppermute | solution.py:272
  42.0 0.7 pad_maximum_fusion.3
  42.7 6.0 %collective-permute-start.1 = (f32[2,8,128]{2,1,0:T(8,128)S(1)}, f32[2,8,128]{2,1,0:T(8,128)S(1)}, u32[]{:S(2)}, u32[]{:S(2)}) collective-permute-start(f32[2,8,128]{2,1,0:T(8,128)S(1)} %pad_maximum_fusion.3), channel_id=1, source_target_pairs={{0,128},{32,160},{64,192},{96,224},{128,0},{160,32},{192,64},{224,... | collective-permute-start | bytes 24584 | tf_op jit(solution)/shard_map/ppermute | solution.py:272
  48.7 3.1 %collective-permute-done.1 = f32[2,8,128]{2,1,0:T(8,128)S(1)} collective-permute-done((f32[2,8,128]{2,1,0:T(8,128)S(1)}, f32[2,8,128]{2,1,0:T(8,128)S(1)}, u32[]{:S(2)}, u32[]{:S(2)}) %collective-permute-start.1) | collective-permute-done | bytes 8224 | tf_op jit(solution)/shard_map/ppermute | solution.py:272
  51.8 1.3 pad_maximum_fusion.2.info_ref
  53.1 9.2 %all-to-all-done = bf16[512,8,128]{2,1,0:T(8,128)(2,1)S(1)} async-done(((bf16[512,8,128]{2,1,0:T(8,128)(2,1)}), bf16[512,8,128]{2,1,0:T(8,128)(2,1)S(1)}, u32[]{:S(2)}, u32[]{:S(2)}) %all-to-all-start) | async-done | bytes 1048608 | tf_op jit(solution)/shard_map/all_to_all | solution.py:267
  62.2 0.0 copy-start
  62.2 1.0 copy-done
  63.2 10.2 %image.1 = (bf16[16,32,8,128]{3,2,1,0:T(8,128)(2,1)}, f32[4,8,128]{2,1,0:T(8,128)}) custom-call(s32[1]{0:T(128)} %bitcast.1.src_ref, f32[4,8,128]{2,1,0:T(8,128)} %pad_maximum_fusion.2.info_ref, bf16[4096,128]{1,0:T(8,128)(2,1)} %bitcast.8, f32[32,1024]{1,0:T(8,128)} %target_ref.1, bf16[1024,1024]{1,0:T(8,128)(2,1)} %get-tuple-element.12.cos_k_ref, ...), custom_call_target="tpu_custom_call" | custom-call | tf_op jit(solution)/shard_map/image/pallas_call | solution.py:317
  73.5 0.0 copy-start.2
  73.5 15.3 %all-to-all-start.1 = ((bf16[512,8,128]{2,1,0:T(8,128)(2,1)}), bf16[512,8,128]{2,1,0:T(8,128)(2,1)S(1)}, u32[]{:S(2)}, u32[]{:S(2)}) async-start(bf16[512,8,128]{2,1,0:T(8,128)(2,1)} %bitcast.10), calls=%async_computation.1 | async-start | bytes 2097152 | tf_op jit(solution)/shard_map/all_to_all | solution.py:267
  88.8 0.0 copy-done.2
  88.8 9.2 %collective-permute-start.2 = (f32[4,8,128]{2,1,0:T(8,128)S(1)}, f32[4,8,128]{2,1,0:T(8,128)S(1)}, u32[]{:S(2)}, u32[]{:S(2)}) collective-permute-start(f32[4,8,128]{2,1,0:T(8,128)S(1)} %copy-done.2), channel_id=1, source_target_pairs={{0,256},{32,288},{64,320},{96,352},{128,384},{160,416},{192,448},{... | collective-permute-start | bytes 49160 | tf_op jit(solution)/shard_map/ppermute | solution.py:272
  98.0 11.3 %collective-permute-done.2 = f32[4,8,128]{2,1,0:T(8,128)S(1)} collective-permute-done((f32[4,8,128]{2,1,0:T(8,128)S(1)}, f32[4,8,128]{2,1,0:T(8,128)S(1)}, u32[]{:S(2)}, u32[]{:S(2)}) %collective-permute-start.2) | collective-permute-done | bytes 16416 | tf_op jit(solution)/shard_map/ppermute | solution.py:272
  109.3 3.1 %collective-permute-start.3 = (f32[8,8,128]{2,1,0:T(8,128)S(1)}, f32[8,8,128]{2,1,0:T(8,128)S(1)}, u32[]{:S(2)}, u32[]{:S(2)}) collective-permute-start(f32[8,8,128]{2,1,0:T(8,128)S(1)} %pad_maximum_fusion.1), channel_id=1, source_target_pairs={{0,32},{32,0},{64,96},{96,64},{128,160},{160,128},{192,224},{224,1... | collective-permute-start | bytes 98312 | tf_op jit(solution)/shard_map/ppermute | solution.py:272
  112.4 0.8 collective-permute-done.3
  113.2 0.6 pad_maximum_fusion.info_ref
  113.8 7.8 %all-to-all-done.1 = bf16[512,8,128]{2,1,0:T(8,128)(2,1)S(1)} async-done(((bf16[512,8,128]{2,1,0:T(8,128)(2,1)}), bf16[512,8,128]{2,1,0:T(8,128)(2,1)S(1)}, u32[]{:S(2)}, u32[]{:S(2)}) %all-to-all-start.1) | async-done | bytes 1048608 | tf_op jit(solution)/shard_map/all_to_all | solution.py:267
  121.6 0.0 copy-start.1
  121.6 1.0 copy-done.1
  122.6 6.4 %gradient.1 = bf16[16,32,128]{2,1,0:T(8,128)(2,1)} custom-call(s32[1]{0:T(128)S(6)} %add.30.place_ref, s32[1]{0:T(128)} %bitcast.1.src_ref, f32[16,8,128]{2,1,0:T(8,128)} %pad_maximum_fusion.info_ref, bf16[4096,128]{1,0:T(8,128)(2,1)} %bitcast.9, bf16[1024,1024]{1,0:T(8,128)(2,1)} %get-tuple-element.18.cos_ref, bf16[1024,1024]{1,0:T(8,128)(2,1)} %get-tuple-element.19.sin_ref), custom_call_target="tpu_custom_call" | custom-call | tf_op jit(solution)/shard_map/gradient/pallas_call | solution.py:341
  128.9 13.9 %all_to_all.15 = bf16[16,32,128]{2,1,0:T(8,128)(2,1)} all-to-all(bf16[16,32,128]{2,1,0:T(8,128)(2,1)} %gradient.1), channel_id=1, replica_groups=mesh['src'=16,'row'=32] {'src'}, dimensions={0} | all-to-all | bytes 262144 | tf_op jit(solution)/shard_map/all_to_all | solution.py:267
  142.9 1.7 %unpack.1 = (f32[32,1024]{1,0:T(8,128)}, f32[32,1024]{1,0:T(8,128)}) custom-call(bf16[512,128]{1,0:T(8,128)(2,1)} %bitcast.11), custom_call_target="tpu_custom_call" | custom-call | tf_op jit(solution)/shard_map/unpack/pallas_call | solution.py:357
  (2 shorter events, 0.0 us)
Async XLA Ops:
  7.2 55.0 %all-to-all-start = ((bf16[512,8,128]{2,1,0:T(8,128)(2,1)}), bf16[512,8,128]{2,1,0:T(8,128)(2,1)S(1)}, u32[]{:S(2)}, u32[]{:S(2)}) async-start(bf16[512,8,128]{2,1,0:T(8,128)(2,1)} %bitcast.7), calls=%async_computation | async-start | bytes 2097152 | tf_op jit(solution)/shard_map/all_to_all | solution.py:267
  35.1 7.0 %collective-permute-start = (f32[1,8,128]{2,1,0:T(8,128)}, f32[1,8,128]{2,1,0:T(8,128)S(1)}, u32[]{:S(2)}, u32[]{:S(2)}) collective-permute-start(f32[1,8,128]{2,1,0:T(8,128)} %get-tuple-element.11), channel_id=1, source_target_pairs={{0,64},{32,96},{64,0},{96,32},{128,192},{160,224},{192,128},{224,1... | collective-permute-start | bytes 12296 | tf_op jit(solution)/shard_map/ppermute | solution.py:272
  42.7 9.0 %collective-permute-start.1 = (f32[2,8,128]{2,1,0:T(8,128)S(1)}, f32[2,8,128]{2,1,0:T(8,128)S(1)}, u32[]{:S(2)}, u32[]{:S(2)}) collective-permute-start(f32[2,8,128]{2,1,0:T(8,128)S(1)} %pad_maximum_fusion.3), channel_id=1, source_target_pairs={{0,128},{32,160},{64,192},{96,224},{128,0},{160,32},{192,64},{224,... | collective-permute-start | bytes 24584 | tf_op jit(solution)/shard_map/ppermute | solution.py:272
  62.2 1.0 copy-start
  73.5 15.3 %copy-start.2 = (f32[4,8,128]{2,1,0:T(8,128)S(1)}, f32[4,8,128]{2,1,0:T(8,128)}, u32[]{:S(2)}) copy-start(f32[4,8,128]{2,1,0:T(8,128)} %get-tuple-element.16) | copy-start | bytes 49156
  73.5 48.2 %all-to-all-start.1 = ((bf16[512,8,128]{2,1,0:T(8,128)(2,1)}), bf16[512,8,128]{2,1,0:T(8,128)(2,1)S(1)}, u32[]{:S(2)}, u32[]{:S(2)}) async-start(bf16[512,8,128]{2,1,0:T(8,128)(2,1)} %bitcast.10), calls=%async_computation.1 | async-start | bytes 2097152 | tf_op jit(solution)/shard_map/all_to_all | solution.py:267
  88.8 20.5 %collective-permute-start.2 = (f32[4,8,128]{2,1,0:T(8,128)S(1)}, f32[4,8,128]{2,1,0:T(8,128)S(1)}, u32[]{:S(2)}, u32[]{:S(2)}) collective-permute-start(f32[4,8,128]{2,1,0:T(8,128)S(1)} %copy-done.2), channel_id=1, source_target_pairs={{0,256},{32,288},{64,320},{96,352},{128,384},{160,416},{192,448},{... | collective-permute-start | bytes 49160 | tf_op jit(solution)/shard_map/ppermute | solution.py:272
  109.3 4.0 %collective-permute-start.3 = (f32[8,8,128]{2,1,0:T(8,128)S(1)}, f32[8,8,128]{2,1,0:T(8,128)S(1)}, u32[]{:S(2)}, u32[]{:S(2)}) collective-permute-start(f32[8,8,128]{2,1,0:T(8,128)S(1)} %pad_maximum_fusion.1), channel_id=1, source_target_pairs={{0,32},{32,0},{64,96},{96,64},{128,160},{160,128},{192,224},{224,1... | collective-permute-start | bytes 98312 | tf_op jit(solution)/shard_map/ppermute | solution.py:272
  121.6 1.0 copy-start.1

commit v6 on v5

--- a/solution.py
+++ b/solution.py
@@ -62,7 +62,7 @@
     return jnp.dot(left, right, preferred_element_type=F32)
 
 
-def spectrum_kernel(row_ref, w_ref, cr_ref, cc_ref, trig_ref, re_ref, im_ref, out_ref, lhs_ref, table_ref, flat_ref):
+def spectrum_kernel(row_ref, w_ref, cr_ref, cc_ref, trig_ref, re_ref, im_ref, out_ref, info_ref, lhs_ref, table_ref, flat_ref):
     step = pl.program_id(0)
     rows, band = re_ref.shape
 
@@ -71,6 +71,7 @@
         spec_re = re_ref[...].astype(F32)
         spec_im = im_ref[...].astype(F32)
         info = info_tile(w_ref, cr_ref, cc_ref)
+        info_ref[0] = info
         centre_row, centre_col = info[:, 1:2], info[:, 2:3]
         col_gap = lax.broadcasted_iota(jnp.int32, (8, band), 1).astype(F32) - centre_col
         col_gap = col_gap * col_gap
@@ -112,12 +113,8 @@
 
 
 def tables_kernel(
-    w_ref, cr_ref, cc_ref, trig_ref, _, info_ref, cos_ref, sin_ref, cos_k_ref, sin_k_ref, cos_y_ref, sin_y_ref
+    trig_ref, _, cos_ref, sin_ref, cos_k_ref, sin_k_ref, cos_y_ref, sin_y_ref
 ):
-    @pl.when(pl.program_id(0) == 0)
-    def _():
-        info_ref[0] = info_tile(w_ref, cr_ref, cc_ref)
-
     base_c, base_s = base_rows(trig_ref, 1.0 / math.sqrt(4 * trig_ref.shape[1]))
     turns = [rotate(pick(trig_ref, 8 + a), pick(trig_ref, 20 + d)) for a in range(8) for d in range(4)]
     turn_c, turn_s = (jnp.concatenate([turn[i] for turn in turns], axis=0) for i in range(2))
@@ -218,7 +215,7 @@
                 out_ref[s, r] = flat_ref[first_row : first_row + 8, :].astype(BF16)
 
 
-def gradient_kernel(place_ref, src_ref, info_ref, in_ref, cos_ref, sin_ref, out_ref, lhs_ref, flat_ref, sums_ref):
+def gradient_kernel(place_ref, src_ref, near_ref, far_ref, in_ref, cos_ref, sin_ref, out_ref, lhs_ref, flat_ref, sums_ref):
     step = pl.program_id(0)
 
     @pl.when(step == 0)
@@ -234,7 +231,7 @@
     by_cos = dot_nn(lhs_ref[...], cos_ref[...])
     by_sin = dot_nn(lhs_ref[...], sin_ref[...])
     gaps = [jnp.bitwise_xor(src_ref[0], s) for s in range(16)]
-    info = jnp.concatenate([info_ref[gap // 2 + 8 * (gap % 2)] for gap in gaps], axis=0)
+    info = jnp.concatenate([jnp.where(gap % 2 == 0, near_ref[gap // 2], far_ref[gap // 2]) for gap in gaps], axis=0)
     root, centre_row, centre_col = info[:, 0:1], info[:, 1:2], info[:, 2:3]
     first_col = (step * CHUNK).astype(F32)
     col_gap = lax.broadcasted_iota(jnp.int32, (LANES, CHUNK), 1).astype(F32) + (first_col - centre_col)
@@ -284,12 +281,12 @@
     col_block = pl.BlockSpec((band, CHUNK), lambda n: (0, n))
     scalars = (weights, cent_row, cent_col)
 
-    column_parts = pl.pallas_call(
+    column_parts, info = pl.pallas_call(
         spectrum_kernel,
         grid=(2,),
         in_specs=[SCALARS, SCALARS, SCALARS, SCALARS, WHOLE, WHOLE, WHOLE],
-        out_specs=pl.BlockSpec((16, 16, 8, LANES), lambda n: (0, n, 0, 0)),
-        out_shape=parts,
+        out_specs=[pl.BlockSpec((16, 16, 8, LANES), lambda n: (0, n, 0, 0)), WHOLE],
+        out_shape=[parts, jax.ShapeDtypeStruct((1, 8, LANES), F32)],
         scratch_shapes=[
             pltpu.VMEM((512, 2 * band), BF16),
             pltpu.VMEM((WIDE, 2 * band), BF16),
@@ -297,22 +294,22 @@
         ],
         name="spectrum",
     )(row, *scalars, trig, spec_re, spec_im)
-    info, cosine, sine, cos_k, sin_k, cos_y, sin_y = pl.pallas_call(
+    cosine, sine, cos_k, sin_k, cos_y, sin_y = pl.pallas_call(
         tables_kernel,
         grid=(STEPS,),
         in_specs=[
-            SCALARS,
-            SCALARS,
-            SCALARS,
             pl.BlockSpec((48, CHUNK), lambda n: (0, n)),
             pl.BlockSpec(memory_space=pl.ANY),
         ],
-        out_specs=[WHOLE] + [col_block] * 6,
-        out_shape=[jax.ShapeDtypeStruct((1, 8, LANES), F32)] + [table] * 6,
+        out_specs=[col_block] * 6,
+        out_shape=[table] * 6,
         cost_estimate=pl.CostEstimate(flops=18 * band * band, bytes_accessed=12 * band * band, transcendentals=0),
         name="tables",
-    )(*scalars, trig, column_parts)
+    )(trig, column_parts)
     some_info = gather_info(info, (2, 4))
+    cosine, sine, cos_k, sin_k, cos_y, sin_y = (
+        pltpu.with_memory_space_constraint(one, pltpu.HBM) for one in (cosine, sine, cos_k, sin_k, cos_y, sin_y)
+    )
     columns = exchange(column_parts.reshape(512, 8, LANES), everyone).reshape(4096, LANES)
     adjoint_parts, some_info = pl.pallas_call(
         image_kernel,
@@ -334,14 +331,16 @@
             pltpu.VMEM((512, band), BF16),
             pltpu.VMEM((4 * WIDE, LANES), F32),
         ],
+        compiler_params=pltpu.CompilerParams(vmem_limit_bytes=40 * 2**20),
         name="image",
     )(src, some_info, columns, target, cos_k, sin_k, cosine, sine)
     adjoint = exchange(adjoint_parts.reshape(512, 8, LANES), everyone).reshape(4096, LANES)
-    all_info = gather_info(some_info, (8, 1))
+    near_info = gather_info(some_info, (8,))
+    far_info = lax.ppermute(near_info, "src", [(i, i ^ 1) for i in range(16)])
     gradient = pl.pallas_call(
         gradient_kernel,
         grid=(STEPS,),
-        in_specs=[SCALARS, SCALARS, WHOLE, WHOLE, col_block, col_block],
+        in_specs=[SCALARS, SCALARS, WHOLE, WHOLE, WHOLE, col_block, col_block],
         out_specs=WHOLE,
         out_shape=jax.ShapeDtypeStruct((16, 32, LANES), BF16),
         scratch_shapes=[
@@ -349,8 +348,9 @@
             pltpu.VMEM((4096, LANES), F32),
             pltpu.VMEM((32, LANES), F32),
         ],
+        compiler_params=pltpu.CompilerParams(vmem_limit_bytes=40 * 2**20),
         name="gradient",
-    )(row * rows + 2 * src, src, all_info, adjoint, cos_y, sin_y)
+    )(row * rows + 2 * src, src, near_info, far_info, adjoint, cos_y, sin_y)
     gradient = exchange(gradient, "src").reshape(512, LANES)
     out = jax.ShapeDtypeStruct((rows, band), F32)
     return tuple(

time: 145 us -> 141 us (0.972)
  waiting for transfers between devices: 35.5 us -> 41.9 us
  starting transfers between devices: 59.3 us -> 55.6 us
  other arithmetic: 4.09 us -> 1.48 us
  local copies, waits for them, and re-layouts: 1.95 us -> 0.02 us
    all_to_all x2, waiting for transfers between devices: 17 us -> 24.2 us  [exchange(): return lax.all_to_all(value, axis, split_axis=0, concat_axis=0, tiled=True)]
    ppermute x4 -> x3, starting transfers between devices: 21.9 us -> 14.8 us  [gather_info(): lax.ppermute(info, 'src', [(i, i ^ bit) for i in range(16)])]
    ppermute x0 -> x1, starting transfers between devices: none -> 3.11 us  [compute(): far_info = lax.ppermute(near_info, 'src', [(i, i ^ 1) for i in range(16)])]
    concatenate x4 -> x2, other arithmetic: 2.62 us -> 0.01 us  [gather_info(): jnp.concatenate([info, lax.ppermute(info, 'src', [(i, i ^ bit) for i in r...]
    unnamed x6 -> x5, local copies, waits for them, and re-layouts: 1.95 us -> 0.01 us
    ppermute x4 -> x3, waiting for transfers between devices: 18.5 us -> 16.9 us  [gather_info(): lax.ppermute(info, 'src', [(i, i ^ bit) for i in range(16)])]
  transfers between devices with their start and end apart: 6 -> 6, of which waited for: 6 -> 5; matrix products, arithmetic and copies ran while one was open for 2% -> 0% of each run, Pallas kernels for 4% -> 4%
where the time goes in v6:
time: 141 us
  starting transfers between devices  55.6 us (39%)
  waiting for transfers between devices  41.9 us (30%)
  Pallas kernels  27.7 us (20%)
  blocking collectives  13 us (9%)
  other arithmetic  1.48 us (1%)
    all_to_all x2, starting transfers between devices, exchange(): return lax.all_to_all(value, axis, split_axis=0, concat_axis=0, tiled=True)  37.8 us
    all_to_all x2, waiting for transfers between devices, exchange(): return lax.all_to_all(value, axis, split_axis=0, concat_axis=0, tiled=True)  24.2 us
    ppermute x3, waiting for transfers between devices, gather_info(): lax.ppermute(info, 'src', [(i, i ^ bit) for i in range(16)])  16.9 us
    ppermute x3, starting transfers between devices, gather_info(): lax.ppermute(info, 'src', [(i, i ^ bit) for i in range(16)])  14.8 us
    all_to_all x1, blocking collectives, exchange(): return lax.all_to_all(value, axis, split_axis=0, concat_axis=0, tiled=True)  13 us
    pallas_call x1, Pallas kernels, compute(): pl.pallas_call(image_kernel, grid=(STEPS + 2,), in_specs=[SCALARS, WHOLE,...  9.7 us
    pallas_call x1, Pallas kernels, compute(): pl.pallas_call(tables_kernel, grid=(STEPS,), in_specs=[pl.BlockSpec((48,...  5.85 us
    pallas_call x1, Pallas kernels, compute(): pl.pallas_call(gradient_kernel, grid=(STEPS,), in_specs=[SCALARS, SCALARS...  5.36 us
  transfers between devices with their start and end apart: 6, of which 5 were waited for; matrix products, arithmetic and copies ran while one was open for 0% of the time, Pallas kernels for 4%

profile of v6, /device:TPU:1, one launch (start us, length us, event | category | flops | bytes accessed | tf_op | source)
XLA Modules:
  0.0 140.5 jit_solution(18411843395509700657)
XLA Ops:
  0.6 0.1 iota_multiply_fusion
  0.7 0.0 copy-start
  0.7 1.4 fusion.3.trig_ref
  2.1 5.1 %spectrum.1 = (bf16[16,32,8,128]{3,2,1,0:T(8,128)(2,1)}, f32[1,8,128]{2,1,0:T(8,128)}) custom-call(s32[1]{0:T(128)} %bitcast.row_ref, f32[8]{0:T(128)} %w_ref.1, s32[8]{0:T(128)} %cr_ref.1, s32[8]{0:T(128)} %cc_ref.1, f32[48,1024]{1,0:T(8,128)} %fusion.3.trig_ref, bf16[32,1024]{1,0:T(8,128)(2,1)} %re_ref.1, bf16[32,1024]{1,0:T(8,128)(2,1)} %im_ref.1), custom_call_target="tpu_custom_call" | custom-call | tf_op jit(solution)/shard_map/spectrum/pallas_call | solution.py:284
  7.2 0.0 copy-start.1
  7.2 22.2 %all-to-all-start = ((bf16[512,8,128]{2,1,0:T(8,128)(2,1)}), bf16[512,8,128]{2,1,0:T(8,128)(2,1)S(1)}, u32[]{:S(2)}, u32[]{:S(2)}) async-start(bf16[512,8,128]{2,1,0:T(8,128)(2,1)} %bitcast.9), calls=%async_computation | async-start | bytes 2097152 | tf_op jit(solution)/shard_map/all_to_all | solution.py:264
  29.4 0.0 copy-done.1
  29.4 3.7 %collective-permute-start = (f32[1,8,128]{2,1,0:T(8,128)S(1)}, f32[1,8,128]{2,1,0:T(8,128)S(1)}, u32[]{:S(2)}, u32[]{:S(2)}) collective-permute-start(f32[1,8,128]{2,1,0:T(8,128)S(1)} %copy-done.1), channel_id=1, source_target_pairs={{0,64},{32,96},{64,0},{96,32},{128,192},{160,224},{192,128},{224,1... | collective-permute-start | bytes 12296 | tf_op jit(solution)/shard_map/ppermute | solution.py:269
  33.1 5.7 %collective-permute-done = f32[1,8,128]{2,1,0:T(8,128)S(1)} collective-permute-done((f32[1,8,128]{2,1,0:T(8,128)S(1)}, f32[1,8,128]{2,1,0:T(8,128)S(1)}, u32[]{:S(2)}, u32[]{:S(2)}) %collective-permute-start) | collective-permute-done | bytes 4128 | tf_op jit(solution)/shard_map/ppermute | solution.py:269
  38.7 1.9 %collective-permute-start.1 = (f32[2,8,128]{2,1,0:T(8,128)S(1)}, f32[2,8,128]{2,1,0:T(8,128)S(1)}, u32[]{:S(2)}, u32[]{:S(2)}) collective-permute-start(f32[2,8,128]{2,1,0:T(8,128)S(1)} %pad_maximum_fusion.1), channel_id=1, source_target_pairs={{0,128},{32,160},{64,192},{96,224},{128,0},{160,32},{192,64},{224,... | collective-permute-start | bytes 24584 | tf_op jit(solution)/shard_map/ppermute | solution.py:269
  40.7 5.8 %tables.1 = (bf16[1024,1024]{1,0:T(8,128)(2,1)}, bf16[1024,1024]{1,0:T(8,128)(2,1)}, bf16[1024,1024]{1,0:T(8,128)(2,1)}, bf16[1024,1024]{1,0:T(8,128)(2,1)}, bf1...) custom-call(f32[48,1024]{1,0:T(8,128)} %fusion.3.trig_ref, bf16[16,32,8,128]{3,2,1,0:T(8,128)(2,1)} %get-tuple-element.13._), custom_call_target="tpu_custom_call" | custom-call | flops 18874368 | bytes 12582912 | tf_op jit(solution)/shard_map/tables/pallas_call | solution.py:297
  46.5 0.0 collective-permute-done.1
  46.5 15.7 %all-to-all-done = bf16[512,8,128]{2,1,0:T(8,128)(2,1)S(1)} async-done(((bf16[512,8,128]{2,1,0:T(8,128)(2,1)}), bf16[512,8,128]{2,1,0:T(8,128)(2,1)S(1)}, u32[]{:S(2)}, u32[]{:S(2)}) %all-to-all-start) | async-done | bytes 1048608 | tf_op jit(solution)/shard_map/all_to_all | solution.py:264
  62.3 0.0 copy-done
  62.3 9.7 %image.1 = (bf16[16,32,8,128]{3,2,1,0:T(8,128)(2,1)}, f32[4,8,128]{2,1,0:T(8,128)S(1)}) custom-call(s32[1]{0:T(128)} %bitcast.1.src_ref, f32[4,8,128]{2,1,0:T(8,128)S(1)} %pad_maximum_fusion.info_ref, bf16[4096,128]{1,0:T(8,128)(2,1)S(1)} %bitcast.7, f32[32,1024]{1,0:T(8,128)S(1)} %copy-done, bf16[1024,1024]{1,0:T(8,128)(2,1)} %get-tuple-element.14.cos_k_ref, ...), custom_call_target="tpu_custom_call" | custom-call | tf_op jit(solution)/shard_map/image/pallas_call | solution.py:314
  72.0 15.6 %all-to-all-start.1 = ((bf16[512,8,128]{2,1,0:T(8,128)(2,1)}), bf16[512,8,128]{2,1,0:T(8,128)(2,1)S(1)}, u32[]{:S(2)}, u32[]{:S(2)}) async-start(bf16[512,8,128]{2,1,0:T(8,128)(2,1)} %bitcast.4), calls=%async_computation.1 | async-start | bytes 2097152 | tf_op jit(solution)/shard_map/all_to_all | solution.py:264
  87.6 9.2 %collective-permute-start.2 = (f32[4,8,128]{2,1,0:T(8,128)S(1)}, f32[4,8,128]{2,1,0:T(8,128)S(1)}, u32[]{:S(2)}, u32[]{:S(2)}) collective-permute-start(f32[4,8,128]{2,1,0:T(8,128)S(1)} %get-tuple-element.18), channel_id=1, source_target_pairs={{0,256},{32,288},{64,320},{96,352},{128,384},{160,416},{192,448},{... | collective-permute-start | bytes 49160 | tf_op jit(solution)/shard_map/ppermute | solution.py:269
  96.8 11.3 %collective-permute-done.2 = f32[4,8,128]{2,1,0:T(8,128)S(1)} collective-permute-done((f32[4,8,128]{2,1,0:T(8,128)S(1)}, f32[4,8,128]{2,1,0:T(8,128)S(1)}, u32[]{:S(2)}, u32[]{:S(2)}) %collective-permute-start.2) | collective-permute-done | bytes 16416 | tf_op jit(solution)/shard_map/ppermute | solution.py:269
  108.1 3.1 %collective-permute-start.3 = (f32[8,8,128]{2,1,0:T(8,128)S(1)}, f32[8,8,128]{2,1,0:T(8,128)S(1)}, u32[]{:S(2)}, u32[]{:S(2)}) collective-permute-start(f32[8,8,128]{2,1,0:T(8,128)S(1)} %constant_dynamic-update-slice_fusion.near_ref), channel_id=1, source_target_pairs={{0,32},{32,0},{64,96},{96,64},{128,160},{160,128},{192,224},{224,1... | collective-permute-start | bytes 98312 | tf_op jit(solution)/shard_map/ppermute | solution.py:339
  111.2 0.8 collective-permute-done.3.far_ref
  112.0 8.4 %all-to-all-done.1 = bf16[512,8,128]{2,1,0:T(8,128)(2,1)S(1)} async-done(((bf16[512,8,128]{2,1,0:T(8,128)(2,1)}), bf16[512,8,128]{2,1,0:T(8,128)(2,1)S(1)}, u32[]{:S(2)}, u32[]{:S(2)}) %all-to-all-start.1) | async-done | bytes 1048608 | tf_op jit(solution)/shard_map/all_to_all | solution.py:264
  120.5 5.4 %gradient.1 = bf16[16,32,128]{2,1,0:T(8,128)(2,1)S(1)} custom-call(s32[1]{0:T(128)S(6)} %add.30.place_ref, s32[1]{0:T(128)} %bitcast.1.src_ref, f32[8,8,128]{2,1,0:T(8,128)S(1)} %constant_dynamic-update-slice_fusion.near_ref, f32[8,8,128]{2,1,0:T(8,128)S(1)} %collective-permute-done.3.far_ref, bf16[4096,128]{1,0:T(8,128)(2,1)S(1)} %bitcast.8, ...), custom_call_target="tpu_custom_call" | custom-call | tf_op jit(solution)/shard_map/gradient/pallas_call | solution.py:340
  125.8 13.0 %all_to_all.15 = bf16[16,32,128]{2,1,0:T(8,128)(2,1)} all-to-all(bf16[16,32,128]{2,1,0:T(8,128)(2,1)S(1)} %gradient.1), channel_id=1, replica_groups=mesh['src'=16,'row'=32] {'src'}, dimensions={0} | all-to-all | bytes 262144 | tf_op jit(solution)/shard_map/all_to_all | solution.py:264
  138.9 1.7 %unpack.1 = (f32[32,1024]{1,0:T(8,128)}, f32[32,1024]{1,0:T(8,128)}) custom-call(bf16[512,128]{1,0:T(8,128)(2,1)} %bitcast.10), custom_call_target="tpu_custom_call" | custom-call | tf_op jit(solution)/shard_map/unpack/pallas_call | solution.py:357
  (5 shorter events, 0.0 us)
Async XLA Ops:
  0.7 61.5 %copy-start = (f32[32,1024]{1,0:T(8,128)S(1)}, f32[32,1024]{1,0:T(8,128)}, u32[]{:S(2)}) copy-start(f32[32,1024]{1,0:T(8,128)} %target_ref.1) | copy-start | bytes 393220
  7.2 22.2 %copy-start.1 = (f32[1,8,128]{2,1,0:T(8,128)S(1)}, f32[1,8,128]{2,1,0:T(8,128)}, u32[]{:S(2)}) copy-start(f32[1,8,128]{2,1,0:T(8,128)} %get-tuple-element.12) | copy-start | bytes 12292
  7.2 55.0 %all-to-all-start = ((bf16[512,8,128]{2,1,0:T(8,128)(2,1)}), bf16[512,8,128]{2,1,0:T(8,128)(2,1)S(1)}, u32[]{:S(2)}, u32[]{:S(2)}) async-start(bf16[512,8,128]{2,1,0:T(8,128)(2,1)} %bitcast.9), calls=%async_computation | async-start | bytes 2097152 | tf_op jit(solution)/shard_map/all_to_all | solution.py:264
  29.4 9.3 %collective-permute-start = (f32[1,8,128]{2,1,0:T(8,128)S(1)}, f32[1,8,128]{2,1,0:T(8,128)S(1)}, u32[]{:S(2)}, u32[]{:S(2)}) collective-permute-start(f32[1,8,128]{2,1,0:T(8,128)S(1)} %copy-done.1), channel_id=1, source_target_pairs={{0,64},{32,96},{64,0},{96,32},{128,192},{160,224},{192,128},{224,1... | collective-permute-start | bytes 12296 | tf_op jit(solution)/shard_map/ppermute | solution.py:269
  38.7 7.8 %collective-permute-start.1 = (f32[2,8,128]{2,1,0:T(8,128)S(1)}, f32[2,8,128]{2,1,0:T(8,128)S(1)}, u32[]{:S(2)}, u32[]{:S(2)}) collective-permute-start(f32[2,8,128]{2,1,0:T(8,128)S(1)} %pad_maximum_fusion.1), channel_id=1, source_target_pairs={{0,128},{32,160},{64,192},{96,224},{128,0},{160,32},{192,64},{224,... | collective-permute-start | bytes 24584 | tf_op jit(solution)/shard_map/ppermute | solution.py:269
  72.0 48.5 %all-to-all-start.1 = ((bf16[512,8,128]{2,1,0:T(8,128)(2,1)}), bf16[512,8,128]{2,1,0:T(8,128)(2,1)S(1)}, u32[]{:S(2)}, u32[]{:S(2)}) async-start(bf16[512,8,128]{2,1,0:T(8,128)(2,1)} %bitcast.4), calls=%async_computation.1 | async-start | bytes 2097152 | tf_op jit(solution)/shard_map/all_to_all | solution.py:264
  87.6 20.5 %collective-permute-start.2 = (f32[4,8,128]{2,1,0:T(8,128)S(1)}, f32[4,8,128]{2,1,0:T(8,128)S(1)}, u32[]{:S(2)}, u32[]{:S(2)}) collective-permute-start(f32[4,8,128]{2,1,0:T(8,128)S(1)} %get-tuple-element.18), channel_id=1, source_target_pairs={{0,256},{32,288},{64,320},{96,352},{128,384},{160,416},{192,448},{... | collective-permute-start | bytes 49160 | tf_op jit(solution)/shard_map/ppermute | solution.py:269
  108.1 4.0 %collective-permute-start.3 = (f32[8,8,128]{2,1,0:T(8,128)S(1)}, f32[8,8,128]{2,1,0:T(8,128)S(1)}, u32[]{:S(2)}, u32[]{:S(2)}) collective-permute-start(f32[8,8,128]{2,1,0:T(8,128)S(1)} %constant_dynamic-update-slice_fusion.near_ref), channel_id=1, source_target_pairs={{0,32},{32,0},{64,96},{96,64},{128,160},{160,128},{192,224},{224,1... | collective-permute-start | bytes 98312 | tf_op jit(solution)/shard_map/ppermute | solution.py:339

commit v7 on v6

--- a/solution.py
+++ b/solution.py
@@ -144,7 +144,6 @@
 
 def image_kernel(
     src_ref,
-    info_ref,
     in_ref,
     target_ref,
     cos_k_ref,
@@ -152,7 +151,6 @@
     cos_ref,
     sin_ref,
     out_ref,
-    info_out_ref,
     lhs_ref,
     grad_ref,
     flat_ref,
@@ -161,7 +159,6 @@
 
     @pl.when(step == 0)
     def _():
-        info_out_ref[...] = info_ref[...]
         for s in range(16):
             turned = in_ref[256 * s : 256 * s + 256, :].T
             for y in range(2):
@@ -230,8 +227,12 @@
 
     by_cos = dot_nn(lhs_ref[...], cos_ref[...])
     by_sin = dot_nn(lhs_ref[...], sin_ref[...])
+
+    def place(gap):
+        return gap % 8
+
     gaps = [jnp.bitwise_xor(src_ref[0], s) for s in range(16)]
-    info = jnp.concatenate([jnp.where(gap % 2 == 0, near_ref[gap // 2], far_ref[gap // 2]) for gap in gaps], axis=0)
+    info = jnp.concatenate([jnp.where(gap < 8, near_ref[place(gap)], far_ref[place(gap)]) for gap in gaps], axis=0)
     root, centre_row, centre_col = info[:, 0:1], info[:, 1:2], info[:, 2:3]
     first_col = (step * CHUNK).astype(F32)
     col_gap = lax.broadcasted_iota(jnp.int32, (LANES, CHUNK), 1).astype(F32) + (first_col - centre_col)
@@ -306,17 +307,16 @@
         cost_estimate=pl.CostEstimate(flops=18 * band * band, bytes_accessed=12 * band * band, transcendentals=0),
         name="tables",
     )(trig, column_parts)
-    some_info = gather_info(info, (2, 4))
+    near_info = gather_info(info, (1, 2, 4))
     cosine, sine, cos_k, sin_k, cos_y, sin_y = (
         pltpu.with_memory_space_constraint(one, pltpu.HBM) for one in (cosine, sine, cos_k, sin_k, cos_y, sin_y)
     )
     columns = exchange(column_parts.reshape(512, 8, LANES), everyone).reshape(4096, LANES)
-    adjoint_parts, some_info = pl.pallas_call(
+    adjoint_parts = pl.pallas_call(
         image_kernel,
         grid=(STEPS + 2,),
         in_specs=[
             SCALARS,
-            WHOLE,
             WHOLE,
             pl.BlockSpec((rows, CHUNK), lambda n: (0, jnp.minimum(n, STEPS - 1))),
             pl.BlockSpec((band, CHUNK), lambda n: (0, jnp.minimum(n, STEPS - 1))),
@@ -324,8 +324,8 @@
             pl.BlockSpec((WIDE, band), lambda n: (jnp.maximum(n - STEPS, 0), 0)),
             pl.BlockSpec((WIDE, band), lambda n: (jnp.maximum(n - STEPS, 0), 0)),
         ],
-        out_specs=[pl.BlockSpec((16, 16, 8, LANES), lambda n: (0, jnp.maximum(n - STEPS, 0), 0, 0)), WHOLE],
-        out_shape=[parts, jax.ShapeDtypeStruct((4, 8, LANES), F32)],
+        out_specs=pl.BlockSpec((16, 16, 8, LANES), lambda n: (0, jnp.maximum(n - STEPS, 0), 0, 0)),
+        out_shape=parts,
         scratch_shapes=[
             pltpu.VMEM((512, band), BF16),
             pltpu.VMEM((512, band), BF16),
@@ -333,10 +333,9 @@
         ],
         compiler_params=pltpu.CompilerParams(vmem_limit_bytes=40 * 2**20),
         name="image",
-    )(src, some_info, columns, target, cos_k, sin_k, cosine, sine)
+    )(src, columns, target, cos_k, sin_k, cosine, sine)
     adjoint = exchange(adjoint_parts.reshape(512, 8, LANES), everyone).reshape(4096, LANES)
-    near_info = gather_info(some_info, (8,))
-    far_info = lax.ppermute(near_info, "src", [(i, i ^ 1) for i in range(16)])
+    far_info = lax.ppermute(near_info, "src", [(i, i ^ 8) for i in range(16)])
     gradient = pl.pallas_call(
         gradient_kernel,
         grid=(STEPS,),

time: 141 us -> 143 us (1.014)
  the two profiles are of different devices: /device:TPU:1 before, /device:TPU:33 now
where the time goes in v7:
time: 143 us
  starting transfers between devices  54.4 us (38%)
  waiting for transfers between devices  39.3 us (27%)
  Pallas kernels  27.8 us (19%)
  blocking collectives  18.8 us (13%)
  other arithmetic  1.48 us (1%)
    all_to_all x2, starting transfers between devices, exchange(): return lax.all_to_all(value, axis, split_axis=0, concat_axis=0, tiled=True)  34.5 us
    all_to_all x2, waiting for transfers between devices, exchange(): return lax.all_to_all(value, axis, split_axis=0, concat_axis=0, tiled=True)  22.9 us
    all_to_all x1, blocking collectives, exchange(): return lax.all_to_all(value, axis, split_axis=0, concat_axis=0, tiled=True)  18.8 us
    ppermute x3, waiting for transfers between devices, gather_info(): lax.ppermute(info, 'src', [(i, i ^ bit) for i in range(16)])  15.1 us
    ppermute x1, starting transfers between devices, compute(): far_info = lax.ppermute(near_info, 'src', [(i, i ^ 8) for i in range(16)])  10.9 us
    pallas_call x1, Pallas kernels, compute(): pl.pallas_call(image_kernel, grid=(STEPS + 2,), in_specs=[SCALARS, WHOLE,...  9.77 us
    ppermute x3, starting transfers between devices, gather_info(): lax.ppermute(info, 'src', [(i, i ^ bit) for i in range(16)])  8.97 us
    pallas_call x1, Pallas kernels, compute(): pl.pallas_call(tables_kernel, grid=(STEPS,), in_specs=[pl.BlockSpec((48,...  5.86 us
  transfers between devices with their start and end apart: 6, of which 5 were waited for; matrix products, arithmetic and copies ran while one was open for 0% of the time, Pallas kernels for 4%

profile of v7, /device:TPU:33, one launch (start us, length us, event | category | flops | bytes accessed | tf_op | source)
XLA Modules:
  0.0 142.5 jit_solution(7338061117273011031)
XLA Ops:
  0.6 0.1 iota_multiply_fusion
  0.7 0.0 copy-start
  0.7 1.4 fusion.3.trig_ref
  2.1 5.2 %spectrum.1 = (bf16[16,32,8,128]{3,2,1,0:T(8,128)(2,1)}, f32[1,8,128]{2,1,0:T(8,128)}) custom-call(s32[1]{0:T(128)} %bitcast.row_ref, f32[8]{0:T(128)} %w_ref.1, s32[8]{0:T(128)} %cr_ref.1, s32[8]{0:T(128)} %cc_ref.1, f32[48,1024]{1,0:T(8,128)} %fusion.3.trig_ref, bf16[32,1024]{1,0:T(8,128)(2,1)} %re_ref.1, bf16[32,1024]{1,0:T(8,128)(2,1)} %im_ref.1), custom_call_target="tpu_custom_call" | custom-call | tf_op jit(solution)/shard_map/spectrum/pallas_call | solution.py:285
  7.3 21.2 %all-to-all-start = ((bf16[512,8,128]{2,1,0:T(8,128)(2,1)}), bf16[512,8,128]{2,1,0:T(8,128)(2,1)S(1)}, u32[]{:S(2)}, u32[]{:S(2)}) async-start(bf16[512,8,128]{2,1,0:T(8,128)(2,1)} %bitcast.9), calls=%async_computation | async-start | bytes 2097152 | tf_op jit(solution)/shard_map/all_to_all | solution.py:265
  28.5 5.9 %tables.1 = (bf16[1024,1024]{1,0:T(8,128)(2,1)}, bf16[1024,1024]{1,0:T(8,128)(2,1)}, bf16[1024,1024]{1,0:T(8,128)(2,1)}, bf16[1024,1024]{1,0:T(8,128)(2,1)}, bf1...) custom-call(f32[48,1024]{1,0:T(8,128)} %fusion.3.trig_ref, bf16[16,32,8,128]{3,2,1,0:T(8,128)(2,1)} %get-tuple-element.11._), custom_call_target="tpu_custom_call" | custom-call | flops 18874368 | bytes 12582912 | tf_op jit(solution)/shard_map/tables/pallas_call | solution.py:298
  34.4 22.9 %all-to-all-done = bf16[512,8,128]{2,1,0:T(8,128)(2,1)S(1)} async-done(((bf16[512,8,128]{2,1,0:T(8,128)(2,1)}), bf16[512,8,128]{2,1,0:T(8,128)(2,1)S(1)}, u32[]{:S(2)}, u32[]{:S(2)}) %all-to-all-start) | async-done | bytes 1048608 | tf_op jit(solution)/shard_map/all_to_all | solution.py:265
  57.3 0.0 copy-done
  57.3 9.8 %image.1 = bf16[16,32,8,128]{3,2,1,0:T(8,128)(2,1)} custom-call(s32[1]{0:T(128)} %bitcast.1.src_ref, bf16[4096,128]{1,0:T(8,128)(2,1)S(1)} %bitcast.8, f32[32,1024]{1,0:T(8,128)S(1)} %copy-done, bf16[1024,1024]{1,0:T(8,128)(2,1)} %get-tuple-element.12.cos_k_ref, bf16[1024,1024]{1,0:T(8,128)(2,1)} %get-tuple-element.13.sin_k_ref, ...), custom_call_target="tpu_custom_call" | custom-call | tf_op jit(solution)/shard_map/image/pallas_call | solution.py:315
  67.1 0.0 copy-start.1
  67.1 13.3 %all-to-all-start.1 = ((bf16[512,8,128]{2,1,0:T(8,128)(2,1)}), bf16[512,8,128]{2,1,0:T(8,128)(2,1)S(1)}, u32[]{:S(2)}, u32[]{:S(2)}) async-start(bf16[512,8,128]{2,1,0:T(8,128)(2,1)} %bitcast.4), calls=%async_computation.1 | async-start | bytes 2097152 | tf_op jit(solution)/shard_map/all_to_all | solution.py:265
  80.4 0.0 copy-done.1
  80.4 2.3 %collective-permute-start = (f32[1,8,128]{2,1,0:T(8,128)S(1)}, f32[1,8,128]{2,1,0:T(8,128)S(1)}, u32[]{:S(2)}, u32[]{:S(2)}) collective-permute-start(f32[1,8,128]{2,1,0:T(8,128)S(1)} %copy-done.1), channel_id=1, source_target_pairs={{0,32},{32,0},{64,96},{96,64},{128,160},{160,128},{192,224},{224,1... | collective-permute-start | bytes 12296 | tf_op jit(solution)/shard_map/ppermute | solution.py:270
  82.7 0.8 collective-permute-done
  83.5 3.6 %collective-permute-start.1 = (f32[2,8,128]{2,1,0:T(8,128)S(1)}, f32[2,8,128]{2,1,0:T(8,128)S(1)}, u32[]{:S(2)}, u32[]{:S(2)}) collective-permute-start(f32[2,8,128]{2,1,0:T(8,128)S(1)} %pad_maximum_fusion.1), channel_id=1, source_target_pairs={{0,64},{32,96},{64,0},{96,32},{128,192},{160,224},{192,128},{224,1... | collective-permute-start | bytes 24584 | tf_op jit(solution)/shard_map/ppermute | solution.py:270
  87.2 11.6 %collective-permute-done.1 = f32[2,8,128]{2,1,0:T(8,128)S(1)} collective-permute-done((f32[2,8,128]{2,1,0:T(8,128)S(1)}, f32[2,8,128]{2,1,0:T(8,128)S(1)}, u32[]{:S(2)}, u32[]{:S(2)}) %collective-permute-start.1) | collective-permute-done | bytes 8224 | tf_op jit(solution)/shard_map/ppermute | solution.py:270
  98.7 3.1 %collective-permute-start.2 = (f32[4,8,128]{2,1,0:T(8,128)S(1)}, f32[4,8,128]{2,1,0:T(8,128)S(1)}, u32[]{:S(2)}, u32[]{:S(2)}) collective-permute-start(f32[4,8,128]{2,1,0:T(8,128)S(1)} %pad_maximum_fusion), channel_id=1, source_target_pairs={{0,128},{32,160},{64,192},{96,224},{128,0},{160,32},{192,64},{224,... | collective-permute-start | bytes 49160 | tf_op jit(solution)/shard_map/ppermute | solution.py:270
  101.8 2.8 %collective-permute-done.2 = f32[4,8,128]{2,1,0:T(8,128)S(1)} collective-permute-done((f32[4,8,128]{2,1,0:T(8,128)S(1)}, f32[4,8,128]{2,1,0:T(8,128)S(1)}, u32[]{:S(2)}, u32[]{:S(2)}) %collective-permute-start.2) | collective-permute-done | bytes 16416 | tf_op jit(solution)/shard_map/ppermute | solution.py:270
  104.6 10.9 %collective-permute-start.3 = (f32[8,8,128]{2,1,0:T(8,128)S(1)}, f32[8,8,128]{2,1,0:T(8,128)S(1)}, u32[]{:S(2)}, u32[]{:S(2)}) collective-permute-start(f32[8,8,128]{2,1,0:T(8,128)S(1)} %constant_dynamic-update-slice_fusion.near_ref), channel_id=1, source_target_pairs={{0,256},{32,288},{64,320},{96,352},{128,384},{160,416},{192,448},{... | collective-permute-start | bytes 98312 | tf_op jit(solution)/shard_map/ppermute | solution.py:338
  115.5 1.3 collective-permute-done.3.far_ref
  116.7 0.0 all-to-all-done.1
  116.7 5.3 %gradient.1 = bf16[16,32,128]{2,1,0:T(8,128)(2,1)S(1)} custom-call(s32[1]{0:T(128)S(6)} %add.30.place_ref, s32[1]{0:T(128)} %bitcast.1.src_ref, f32[8,8,128]{2,1,0:T(8,128)S(1)} %constant_dynamic-update-slice_fusion.near_ref, f32[8,8,128]{2,1,0:T(8,128)S(1)} %collective-permute-done.3.far_ref, bf16[4096,128]{1,0:T(8,128)(2,1)S(1)} %bitcast.7, ...), custom_call_target="tpu_custom_call" | custom-call | tf_op jit(solution)/shard_map/gradient/pallas_call | solution.py:339
  122.1 18.8 %all_to_all.15 = bf16[16,32,128]{2,1,0:T(8,128)(2,1)} all-to-all(bf16[16,32,128]{2,1,0:T(8,128)(2,1)S(1)} %gradient.1), channel_id=1, replica_groups=mesh['src'=16,'row'=32] {'src'}, dimensions={0} | all-to-all | bytes 262144 | tf_op jit(solution)/shard_map/all_to_all | solution.py:265
  140.9 1.7 %unpack.1 = (f32[32,1024]{1,0:T(8,128)}, f32[32,1024]{1,0:T(8,128)}) custom-call(bf16[512,128]{1,0:T(8,128)(2,1)} %bitcast.10), custom_call_target="tpu_custom_call" | custom-call | tf_op jit(solution)/shard_map/unpack/pallas_call | solution.py:356
  (7 shorter events, 0.0 us)
Async XLA Ops:
  0.7 56.6 %copy-start = (f32[32,1024]{1,0:T(8,128)S(1)}, f32[32,1024]{1,0:T(8,128)}, u32[]{:S(2)}) copy-start(f32[32,1024]{1,0:T(8,128)} %target_ref.1) | copy-start | bytes 393220
  7.3 50.0 %all-to-all-start = ((bf16[512,8,128]{2,1,0:T(8,128)(2,1)}), bf16[512,8,128]{2,1,0:T(8,128)(2,1)S(1)}, u32[]{:S(2)}, u32[]{:S(2)}) async-start(bf16[512,8,128]{2,1,0:T(8,128)(2,1)} %bitcast.9), calls=%async_computation | async-start | bytes 2097152 | tf_op jit(solution)/shard_map/all_to_all | solution.py:265
  67.1 13.3 %copy-start.1 = (f32[1,8,128]{2,1,0:T(8,128)S(1)}, f32[1,8,128]{2,1,0:T(8,128)}, u32[]{:S(2)}) copy-start(f32[1,8,128]{2,1,0:T(8,128)} %get-tuple-element.10) | copy-start | bytes 12292
  67.1 49.7 %all-to-all-start.1 = ((bf16[512,8,128]{2,1,0:T(8,128)(2,1)}), bf16[512,8,128]{2,1,0:T(8,128)(2,1)S(1)}, u32[]{:S(2)}, u32[]{:S(2)}) async-start(bf16[512,8,128]{2,1,0:T(8,128)(2,1)} %bitcast.4), calls=%async_computation.1 | async-start | bytes 2097152 | tf_op jit(solution)/shard_map/all_to_all | solution.py:265
  80.4 3.1 %collective-permute-start = (f32[1,8,128]{2,1,0:T(8,128)S(1)}, f32[1,8,128]{2,1,0:T(8,128)S(1)}, u32[]{:S(2)}, u32[]{:S(2)}) collective-permute-start(f32[1,8,128]{2,1,0:T(8,128)S(1)} %copy-done.1), channel_id=1, source_target_pairs={{0,32},{32,0},{64,96},{96,64},{128,160},{160,128},{192,224},{224,1... | collective-permute-start | bytes 12296 | tf_op jit(solution)/shard_map/ppermute | solution.py:270
  83.5 15.2 %collective-permute-start.1 = (f32[2,8,128]{2,1,0:T(8,128)S(1)}, f32[2,8,128]{2,1,0:T(8,128)S(1)}, u32[]{:S(2)}, u32[]{:S(2)}) collective-permute-start(f32[2,8,128]{2,1,0:T(8,128)S(1)} %pad_maximum_fusion.1), channel_id=1, source_target_pairs={{0,64},{32,96},{64,0},{96,32},{128,192},{160,224},{192,128},{224,1... | collective-permute-start | bytes 24584 | tf_op jit(solution)/shard_map/ppermute | solution.py:270
  98.7 5.8 %collective-permute-start.2 = (f32[4,8,128]{2,1,0:T(8,128)S(1)}, f32[4,8,128]{2,1,0:T(8,128)S(1)}, u32[]{:S(2)}, u32[]{:S(2)}) collective-permute-start(f32[4,8,128]{2,1,0:T(8,128)S(1)} %pad_maximum_fusion), channel_id=1, source_target_pairs={{0,128},{32,160},{64,192},{96,224},{128,0},{160,32},{192,64},{224,... | collective-permute-start | bytes 49160 | tf_op jit(solution)/shard_map/ppermute | solution.py:270
  104.6 12.2 %collective-permute-start.3 = (f32[8,8,128]{2,1,0:T(8,128)S(1)}, f32[8,8,128]{2,1,0:T(8,128)S(1)}, u32[]{:S(2)}, u32[]{:S(2)}) collective-permute-start(f32[8,8,128]{2,1,0:T(8,128)S(1)} %constant_dynamic-update-slice_fusion.near_ref), channel_id=1, source_target_pairs={{0,256},{32,288},{64,320},{96,352},{128,384},{160,416},{192,448},{... | collective-permute-start | bytes 98312 | tf_op jit(solution)/shard_map/ppermute | solution.py:338
